TPU v7x, 512 devices: a whole 4x4x16 slice. The times are simulated.
512 devices in a mesh: gz: 4 (over y), gy: 4 (over x_lo, core), col: 32 (over z, x_hi).
Axes of the slice: x: 4 (x_hi: 2, x_lo: 2; x = x_hi * 2 + x_lo), y: 4, z: 16, core: 2. Of those that a mesh axis runs over, the one named last changes fastest.
Arguments:
- volume: bfloat16 [8, 8, 1024, 128], P('gz', 'gy', 'col'), may hold values from -6 to 6
- conv_weight: bfloat16 [27, 2, 1024, 1024], P(None, None, 'col'), may hold values from -0.0390625 to 0.0390625
- proj_weight: bfloat16 [1024, 512], replicated, may hold values from -0.1875 to 0.1875
Outputs:
- fine_tiles: float32 [32, 32, 4096], P('gz', 'gy', 'col')
All inputs are finite; a program needn't handle non-finite values.
Results may differ from a plain program's by a relative error of at most 0.0029.
Values may be sent and summed in bfloat16 or wider, within the bound.
No kernel may reach another device: no remote copies, remote signals or barrier semaphores. Data moves between devices by JAX's collectives and lax.ppermute only.
A program may use at most 64 MiB of HBM per device.

v0:
```python
import jax
import jax.numpy as jnp
from jax import lax
from jax.sharding import PartitionSpec as P


def extended(cells, sides, width, closed):
    for axis, dim in sides:
        count = lax.axis_size(axis)
        ends = count if closed else count - 1
        head = lax.slice_in_dim(cells, 0, width, axis=dim)
        tail = lax.slice_in_dim(cells, cells.shape[dim] - width, cells.shape[dim], axis=dim)
        cells = jnp.concatenate(
            [
                lax.ppermute(tail, axis, [(i, (i + 1) % count) for i in range(ends)]),
                cells,
                lax.ppermute(head, axis, [((i + 1) % count, i) for i in range(ends)]),
            ],
            axis=dim,
        )
    return cells


def inverse_lift(low_band, high_band, along):
    length = low_band.shape[along]

    def window_of(array, first, last):
        return lax.slice_in_dim(array, first, last, axis=along)

    even_rows = window_of(low_band, 1, length - 1) - 0.25 * (
        window_of(high_band, 0, length - 2) + window_of(high_band, 1, length - 1)
    )
    next_even = window_of(low_band, 2, length) - 0.25 * (
        window_of(high_band, 1, length - 1) + window_of(high_band, 2, length)
    )
    odd_rows = window_of(high_band, 1, length - 1) + 0.5 * (even_rows + next_even)
    paired = jnp.stack([even_rows, odd_rows], axis=along + 1)
    new_shape = list(even_rows.shape)
    new_shape[along] = 2 * (length - 2)
    return paired.reshape(new_shape)


def synthesize(coefficients):
    quarter = coefficients.shape[-1] // 4
    bands = coefficients.reshape(coefficients.shape[:-1] + (4, quarter))
    low_z = inverse_lift(bands[..., 0, :], bands[..., 2, :], 0)
    high_z = inverse_lift(bands[..., 1, :], bands[..., 3, :], 0)
    return inverse_lift(low_z, high_z, 1)


def convolve(brick_data, tap_weights):
    kernel = tap_weights.reshape(
        (3, 3, 3, tap_weights.shape[1] * tap_weights.shape[2], tap_weights.shape[3])
    )
    result = lax.conv_general_dilated(
        brick_data[None],
        kernel,
        (1, 1, 1),
        ((0, 0), (0, 0), (1, 1)),
        dimension_numbers=("NDHCW", "DHWOI", "NDHCW"),
        preferred_element_type=jnp.float32,
    )
    return result[0]


def on_device(volume, conv_weight, proj_weight):
    out_width = conv_weight.shape[2]
    with_faces = extended(volume, (("gz", 0), ("gy", 1)), 1, False)
    zero_sum = jnp.zeros(
        (volume.shape[0], volume.shape[1], 2 * out_width, volume.shape[3]), jnp.float32
    )
    conv_out = zero_sum + convolve(
        lax.all_gather(with_faces, "col", axis=2, tiled=True), conv_weight
    )
    gated_values = (
        jax.nn.silu(conv_out[:, :, :out_width, :]) * conv_out[:, :, out_width:, :]
    ).astype(jnp.bfloat16)
    coefficients = jnp.einsum(
        "zycx,cp->zyxp",
        lax.all_to_all(gated_values, "col", split_axis=3, concat_axis=2, tiled=True),
        proj_weight,
        preferred_element_type=jnp.float32,
    )
    coarse = extended(coefficients, (("gz", 0), ("gy", 1)), 1, True)
    middle = synthesize(coarse)
    middle_rims = extended(middle, (("gz", 0), ("gy", 1)), 1, True)
    fine_tiles = synthesize(middle_rims)
    return fine_tiles.reshape(
        (fine_tiles.shape[0], fine_tiles.shape[1], fine_tiles.shape[2] * fine_tiles.shape[3])
    )


def solution(mesh):
    return jax.shard_map(
        on_device,
        mesh=mesh,
        in_specs=(P("gz", "gy", "col", None), P(None, None, "col", None), P()),
        out_specs=P("gz", "gy", "col"),
        check_vma=False,
    )
```

profile of v0, /device:TPU:1, one launch (start us, length us, event | category | flops | bytes accessed | tf_op | source)
XLA Modules:
  0.0 309.3 jit_solution(12510811969379018881)
XLA Ops:
  7.4 4.1 %collective-permute-start = (bf16[1,2,32,128]{3,2,1,0:T(8,128)(2,1)S(1)}, bf16[1,2,32,128]{3,2,1,0:T(8,128)(2,1)S(1)}, u32[]{:S(2)}, u32[]{:S(2)}) collective-permute-start(bf16[1,2,32,128]{3,2,1,0:T(8,128)(2,1)S(1)} %get-tuple-element.48), channel_id=1, source_target_pairs={{0,128},{128,256},{256,384},{1,129},{129,257},{257,385},{2,130},{1... | collective-permute-start | bytes 49160 | tf_op jit(solution)/shard_map/ppermute | solution.py:15
  13.7 2.4 collective-permute-done.1
  16.1 5.1 %collective-permute-start.2 = (bf16[4,1,32,128]{3,2,1,0:T(8,128)(2,1)S(1)}, bf16[4,1,32,128]{3,2,1,0:T(8,128)(2,1)S(1)}, u32[]{:S(2)}, u32[]{:S(2)}) collective-permute-start(bf16[4,1,32,128]{3,2,1,0:T(8,128)(2,1)S(1)} %get-tuple-element.39), channel_id=1, source_target_pairs={{0,32},{32,64},{64,96},{1,33},{33,65},{65,97},{2,34},{34,66},{66,9... | collective-permute-start | bytes 98312 | tf_op jit(solution)/shard_map/ppermute | solution.py:15
  21.2 3.4 %collective-permute-start.3 = (bf16[4,1,32,128]{3,2,1,0:T(8,128)(2,1)S(1)}, bf16[4,1,32,128]{3,2,1,0:T(8,128)(2,1)S(1)}, u32[]{:S(2)}, u32[]{:S(2)}) collective-permute-start(bf16[4,1,32,128]{3,2,1,0:T(8,128)(2,1)S(1)} %get-tuple-element.40), channel_id=1, source_target_pairs={{32,0},{64,32},{96,64},{33,1},{65,33},{97,65},{34,2},{66,34},{98,6... | collective-permute-start | bytes 98312 | tf_op jit(solution)/shard_map/ppermute | solution.py:17
  24.6 1.9 collective-permute-done.3
  27.1 159.2 %all-gather.2.cloned.1.call-done = bf16[4,4,1024,128]{3,2,1,0:T(8,128)(2,1)} async-done(((bf16[4,4,32,128]{3,2,1,0:T(8,128)(2,1)}), bf16[4,4,1024,128]{3,2,1,0:T(8,128)(2,1)}) %all-gather.2.cloned.1.call-update) | async-done | bytes 4194320 | tf_op jit(solution)/shard_map/all_gather | solution.py:73
  186.3 7.9 %copy.198 = bf16[4,4,1024,1,128]{2,1,4,0,3:T(4,128)(2,1)} copy(bf16[4,4,1024,1,128]{4,2,1,0,3:T(8,128)(2,1)} %bitcast.103) | data formatting | bytes 8388608
  194.2 3.9 %pad.clone = bf16[4,4,1024,1,136]{2,1,4,0,3:T(4,128)(2,1)S(1)} pad(bf16[4,4,1024,1,128]{2,1,4,0,3:T(4,128)(2,1)} %copy.198, bf16[]{:T(256)} %constant.2), padding=0_0x0_0x0_0x0_0x1_7 | pad | bytes 8650754 | tf_op jit(solution)/shard_map/broadcast_in_dim | solution.py:56
  199.8 7.9 %fusion.9 = f32[2,2,8,17,64]{4,2,3,1,0:T(8,128)S(1)} fusion(bf16[3,3,3,64,1024]{4,3,2,1,0:T(8,128)(2,1)S(1)} %bitcast.101, bf16[4,4,1024,1,7,2]{2,4,5,1,0,3:T(8,128)(2,1)S(1)} %slice.308, bf16[4,4,1024,1,8,17]{2,4,5,1,0,3:T(8,128)(2,1)S(1)} %copy.146, pred[8,17]{0,1:T(8,128)(4,1)S(1)} %copy-done.1), kind=kOutput, calls=%fused_computation.9 | convolution fusion | flops 1940162560 | bytes 8593544 | tf_op jit(solution)/shard_map/conv_general_dilated | solution.py:55
  208.6 1.7 copy.178
  215.0 21.0 %all_to_all.18 = bf16[32,2,256]{2,1,0:T(2,128)(2,1)} all-to-all(bf16[32,2,256]{2,1,0:T(2,128)(2,1)} %reshape.411), channel_id=1, replica_groups=mesh['gz'=4,'gy'=4,'col'=32] {'col'}, dimensions={0} | all-to-all | bytes 65536 | tf_op jit(solution)/shard_map/all_to_all | solution.py:80
  242.4 3.1 %collective-permute-start.4 = (f32[1,2,4,512]{3,2,1,0:T(4,128)S(1)}, f32[1,2,4,512]{3,2,1,0:T(4,128)S(1)}, u32[]{:S(2)}, u32[]{:S(2)}) collective-permute-start(f32[1,2,4,512]{3,2,1,0:T(4,128)S(1)} %get-tuple-element.45), channel_id=1, source_target_pairs={{0,128},{128,256},{256,384},{384,0},{1,129},{129,257},{257,385},{3... | collective-permute-start | bytes 49160 | tf_op jit(solution)/shard_map/ppermute | solution.py:15
  245.6 3.4 %collective-permute-start.5 = (f32[1,2,4,512]{3,2,1,0:T(4,128)S(1)}, f32[1,2,4,512]{3,2,1,0:T(4,128)S(1)}, u32[]{:S(2)}, u32[]{:S(2)}) collective-permute-start(f32[1,2,4,512]{3,2,1,0:T(4,128)S(1)} %get-tuple-element.46), channel_id=1, source_target_pairs={{128,0},{256,128},{384,256},{0,384},{129,1},{257,129},{385,257},{1... | collective-permute-start | bytes 49160 | tf_op jit(solution)/shard_map/ppermute | solution.py:17
  250.1 16.8 %collective-permute-start.6 = (f32[4,1,4,512]{3,2,1,0:T(4,128)S(1)}, f32[4,1,4,512]{3,2,1,0:T(4,128)S(1)}, u32[]{:S(2)}, u32[]{:S(2)}) collective-permute-start(f32[4,1,4,512]{3,2,1,0:T(4,128)S(1)} %get-tuple-element.37), channel_id=1, source_target_pairs={{0,32},{32,64},{64,96},{96,0},{1,33},{33,65},{65,97},{97,1},{2,34}... | collective-permute-start | bytes 98312 | tf_op jit(solution)/shard_map/ppermute | solution.py:15
  266.9 1.9 collective-permute-start.7
  268.8 3.3 %collective-permute-done.7 = f32[4,1,4,512]{3,2,1,0:T(4,128)S(1)} collective-permute-done((f32[4,1,4,512]{3,2,1,0:T(4,128)S(1)}, f32[4,1,4,512]{3,2,1,0:T(4,128)S(1)}, u32[]{:S(2)}, u32[]{:S(2)}) %collective-permute-start.7) | collective-permute-done | bytes 32800 | tf_op jit(solution)/shard_map/ppermute | solution.py:17
  276.1 4.6 %collective-permute-start.9 = (f32[1,4,4,128]{3,2,1,0:T(4,128)S(1)}, f32[1,4,4,128]{3,2,1,0:T(4,128)S(1)}, u32[]{:S(2)}, u32[]{:S(2)}) collective-permute-start(f32[1,4,4,128]{3,2,1,0:T(4,128)S(1)} %bitcast.136), channel_id=1, source_target_pairs={{128,0},{256,128},{384,256},{0,384},{129,1},{257,129},{385,257},{1... | collective-permute-start | bytes 24584 | tf_op jit(solution)/shard_map/ppermute | solution.py:17
  280.7 1.9 collective-permute-start.8
  282.6 3.6 %collective-permute-done.8 = f32[1,4,4,128]{3,2,1,0:T(4,128)S(1)} collective-permute-done((f32[1,4,4,128]{3,2,1,0:T(4,128)S(1)}, f32[1,4,4,128]{3,2,1,0:T(4,128)S(1)}, u32[]{:S(2)}, u32[]{:S(2)}) %collective-permute-start.8) | collective-permute-done | bytes 8224 | tf_op jit(solution)/shard_map/ppermute | solution.py:15
  286.3 3.3 %collective-permute-start.10 = (f32[6,1,4,128]{3,2,1,0:T(4,128)S(1)}, f32[6,1,4,128]{3,2,1,0:T(4,128)S(1)}, u32[]{:S(2)}, u32[]{:S(2)}) collective-permute-start(f32[6,1,4,128]{3,2,1,0:T(4,128)S(1)} %get-tuple-element.41), channel_id=1, source_target_pairs={{0,32},{32,64},{64,96},{96,0},{1,33},{33,65},{65,97},{97,1},{2,34}... | collective-permute-start | bytes 36872 | tf_op jit(solution)/shard_map/ppermute | solution.py:15
  289.6 1.9 collective-permute-start.11
  291.6 3.1 collective-permute-done.11
  295.3 1.8 reshape.395
  297.1 2.7 fusion.38
  (60 shorter events, 25.6 us)
Async XLA Ops:
  6.5 193.2 %copy-start = (bf16[27,2,32,1024]{3,2,1,0:T(8,128)(2,1)S(1)}, bf16[27,2,32,1024]{3,2,1,0:T(8,128)(2,1)}, u32[]{:S(2)}) copy-start(bf16[27,2,32,1024]{3,2,1,0:T(8,128)(2,1)} %param.4) | copy-start | bytes 10616836
  6.5 179.8 %all-gather.2.cloned.1.call-start = ((), (), s32[]{:S(2)}) async-start(), calls=%async_computation.1 | async-start | bytes 4325376 | tf_op jit(solution)/shard_map/all_gather | solution.py:73
  7.4 5.4 %collective-permute-start = (bf16[1,2,32,128]{3,2,1,0:T(8,128)(2,1)S(1)}, bf16[1,2,32,128]{3,2,1,0:T(8,128)(2,1)S(1)}, u32[]{:S(2)}, u32[]{:S(2)}) collective-permute-start(bf16[1,2,32,128]{3,2,1,0:T(8,128)(2,1)S(1)} %get-tuple-element.48), channel_id=1, source_target_pairs={{0,128},{128,256},{256,384},{1,129},{129,257},{257,385},{2,130},{1... | collective-permute-start | bytes 49160 | tf_op jit(solution)/shard_map/ppermute | solution.py:15
  11.6 4.5 %collective-permute-start.1 = (bf16[1,2,32,128]{3,2,1,0:T(8,128)(2,1)S(1)}, bf16[1,2,32,128]{3,2,1,0:T(8,128)(2,1)S(1)}, u32[]{:S(2)}, u32[]{:S(2)}) collective-permute-start(bf16[1,2,32,128]{3,2,1,0:T(8,128)(2,1)S(1)} %get-tuple-element.47), channel_id=1, source_target_pairs={{128,0},{256,128},{384,256},{129,1},{257,129},{385,257},{130,2},{2... | collective-permute-start | bytes 49160 | tf_op jit(solution)/shard_map/ppermute | solution.py:17
  16.1 8.5 %collective-permute-start.2 = (bf16[4,1,32,128]{3,2,1,0:T(8,128)(2,1)S(1)}, bf16[4,1,32,128]{3,2,1,0:T(8,128)(2,1)S(1)}, u32[]{:S(2)}, u32[]{:S(2)}) collective-permute-start(bf16[4,1,32,128]{3,2,1,0:T(8,128)(2,1)S(1)} %get-tuple-element.39), channel_id=1, source_target_pairs={{0,32},{32,64},{64,96},{1,33},{33,65},{65,97},{2,34},{34,66},{66,9... | collective-permute-start | bytes 98312 | tf_op jit(solution)/shard_map/ppermute | solution.py:15
  21.2 5.2 %collective-permute-start.3 = (bf16[4,1,32,128]{3,2,1,0:T(8,128)(2,1)S(1)}, bf16[4,1,32,128]{3,2,1,0:T(8,128)(2,1)S(1)}, u32[]{:S(2)}, u32[]{:S(2)}) collective-permute-start(bf16[4,1,32,128]{3,2,1,0:T(8,128)(2,1)S(1)} %get-tuple-element.40), channel_id=1, source_target_pairs={{32,0},{64,32},{96,64},{33,1},{65,33},{97,65},{34,2},{66,34},{98,6... | collective-permute-start | bytes 98312 | tf_op jit(solution)/shard_map/ppermute | solution.py:17
  198.1 1.7 copy-start.1
  242.4 6.5 %collective-permute-start.4 = (f32[1,2,4,512]{3,2,1,0:T(4,128)S(1)}, f32[1,2,4,512]{3,2,1,0:T(4,128)S(1)}, u32[]{:S(2)}, u32[]{:S(2)}) collective-permute-start(f32[1,2,4,512]{3,2,1,0:T(4,128)S(1)} %get-tuple-element.45), channel_id=1, source_target_pairs={{0,128},{128,256},{256,384},{384,0},{1,129},{129,257},{257,385},{3... | collective-permute-start | bytes 49160 | tf_op jit(solution)/shard_map/ppermute | solution.py:15
  245.6 4.5 %collective-permute-start.5 = (f32[1,2,4,512]{3,2,1,0:T(4,128)S(1)}, f32[1,2,4,512]{3,2,1,0:T(4,128)S(1)}, u32[]{:S(2)}, u32[]{:S(2)}) collective-permute-start(f32[1,2,4,512]{3,2,1,0:T(4,128)S(1)} %get-tuple-element.46), channel_id=1, source_target_pairs={{128,0},{256,128},{384,256},{0,384},{129,1},{257,129},{385,257},{1... | collective-permute-start | bytes 49160 | tf_op jit(solution)/shard_map/ppermute | solution.py:17
  250.1 18.7 %collective-permute-start.6 = (f32[4,1,4,512]{3,2,1,0:T(4,128)S(1)}, f32[4,1,4,512]{3,2,1,0:T(4,128)S(1)}, u32[]{:S(2)}, u32[]{:S(2)}) collective-permute-start(f32[4,1,4,512]{3,2,1,0:T(4,128)S(1)} %get-tuple-element.37), channel_id=1, source_target_pairs={{0,32},{32,64},{64,96},{96,0},{1,33},{33,65},{65,97},{97,1},{2,34}... | collective-permute-start | bytes 98312 | tf_op jit(solution)/shard_map/ppermute | solution.py:15
  266.9 5.2 %collective-permute-start.7 = (f32[4,1,4,512]{3,2,1,0:T(4,128)S(1)}, f32[4,1,4,512]{3,2,1,0:T(4,128)S(1)}, u32[]{:S(2)}, u32[]{:S(2)}) collective-permute-start(f32[4,1,4,512]{3,2,1,0:T(4,128)S(1)} %get-tuple-element.38), channel_id=1, source_target_pairs={{32,0},{64,32},{96,64},{0,96},{33,1},{65,33},{97,65},{1,97},{34,2}... | collective-permute-start | bytes 98312 | tf_op jit(solution)/shard_map/ppermute | solution.py:17
  276.1 6.6 %collective-permute-start.9 = (f32[1,4,4,128]{3,2,1,0:T(4,128)S(1)}, f32[1,4,4,128]{3,2,1,0:T(4,128)S(1)}, u32[]{:S(2)}, u32[]{:S(2)}) collective-permute-start(f32[1,4,4,128]{3,2,1,0:T(4,128)S(1)} %bitcast.136), channel_id=1, source_target_pairs={{128,0},{256,128},{384,256},{0,384},{129,1},{257,129},{385,257},{1... | collective-permute-start | bytes 24584 | tf_op jit(solution)/shard_map/ppermute | solution.py:17
  280.7 5.6 %collective-permute-start.8 = (f32[1,4,4,128]{3,2,1,0:T(4,128)S(1)}, f32[1,4,4,128]{3,2,1,0:T(4,128)S(1)}, u32[]{:S(2)}, u32[]{:S(2)}) collective-permute-start(f32[1,4,4,128]{3,2,1,0:T(4,128)S(1)} %bitcast.135), channel_id=1, source_target_pairs={{0,128},{128,256},{256,384},{384,0},{1,129},{129,257},{257,385},{3... | collective-permute-start | bytes 24584 | tf_op jit(solution)/shard_map/ppermute | solution.py:15
  286.3 5.3 %collective-permute-start.10 = (f32[6,1,4,128]{3,2,1,0:T(4,128)S(1)}, f32[6,1,4,128]{3,2,1,0:T(4,128)S(1)}, u32[]{:S(2)}, u32[]{:S(2)}) collective-permute-start(f32[6,1,4,128]{3,2,1,0:T(4,128)S(1)} %get-tuple-element.41), channel_id=1, source_target_pairs={{0,32},{32,64},{64,96},{96,0},{1,33},{33,65},{65,97},{97,1},{2,34}... | collective-permute-start | bytes 36872 | tf_op jit(solution)/shard_map/ppermute | solution.py:15
  289.6 5.0 %collective-permute-start.11 = (f32[6,1,4,128]{3,2,1,0:T(4,128)S(1)}, f32[6,1,4,128]{3,2,1,0:T(4,128)S(1)}, u32[]{:S(2)}, u32[]{:S(2)}) collective-permute-start(f32[6,1,4,128]{3,2,1,0:T(4,128)S(1)} %get-tuple-element.42), channel_id=1, source_target_pairs={{32,0},{64,32},{96,64},{0,96},{33,1},{65,33},{97,65},{1,97},{34,2}... | collective-permute-start | bytes 36872 | tf_op jit(solution)/shard_map/ppermute | solution.py:17
Sparse Core Ops, SparseCore 0:
  27.2 159.0 all-gather.1
where the time goes:
time: 310 us; the launch traced here: 309 us
  waiting for transfers between devices  175 us (56%)
  starting transfers between devices  50.9 us (16%)
  local copies, waits for them, and re-layouts  35.8 us (12%)
  blocking collectives  21 us (7%)
  between operations  13.8 us (4%)
  matrix products  9.42 us (3%)
  other arithmetic  3.83 us (1%)
    all_gather x1, waiting for transfers between devices, on_device(): lax.all_gather(with_faces, 'col', axis=2, tiled=True)  159 us
    ppermute x6, starting transfers between devices, extended(): lax.ppermute(tail, axis, [(i, (i + 1) % count) for i in range(ends)])  34.4 us
    all_to_all x1, blocking collectives, on_device(): lax.all_to_all(gated_values, 'col', split_axis=3, concat_axis=2, tiled=True)  21 us
    ppermute x6, starting transfers between devices, extended(): lax.ppermute(head, axis, [((i + 1) % count, i) for i in range(ends)])  16.5 us
    unnamed x10, local copies, waits for them, and re-layouts  13.6 us
    ppermute x6, waiting for transfers between devices, extended(): lax.ppermute(head, axis, [((i + 1) % count, i) for i in range(ends)])  11.7 us
    conv_general_dilated x1, matrix products, convolve(): lax.conv_general_dilated(brick_data[None], kernel, (1, 1, 1), ((0, 0), (0...  7.92 us
  transfers between devices with their start and end apart: 13, of which 7 were waited for; matrix products, arithmetic and copies ran while one was open for 0% of the time, Pallas kernels for 0%

commit v1 on v0

v1 whole, which is shorter than its diff:
```python
import jax
import jax.numpy as jnp
from jax import lax
from jax.experimental import pallas as pl
from jax.experimental.pallas import tpu as pltpu
from jax.sharding import Mesh, PartitionSpec as P

F32 = jnp.float32
BF16 = jnp.bfloat16
VMEM = pl.BlockSpec(memory_space=pltpu.VMEM)
SMEM = pl.BlockSpec(memory_space=pltpu.SMEM)


def conv_kernel(half_ref, own_ref, other_ref, weight_ref, low_ref, inner_ref, high_ref, cells, total):
    step = pl.program_id(0)

    @pl.when(step == 0)
    def _():
        half = half_ref[0]
        for k in range(16):
            for row in range(4):
                lanes = pl.ds(row * 128, 128)
                cells[k, half, :, lanes] = own_ref[k, row]
                cells[k, 1 - half, :, lanes] = other_ref[k, row]
        total[...] = jnp.zeros_like(total)

    products = jnp.dot(
        weight_ref[0], cells[...].reshape(1024, 512), preferred_element_type=F32
    )
    lane = lax.broadcasted_iota(jnp.int32, (64, 128), 1)
    for dy in range(3):
        for z in range(2):
            for y in range(2):
                row = z * 2 + y
                before, centre, after = (
                    products[(dy * 3 + dx) * 64 : (dy * 3 + dx + 1) * 64, row * 128 : (row + 1) * 128]
                    for dx in range(3)
                )
                term = (
                    centre
                    + jnp.where(lane == 0, 0.0, pltpu.roll(before, 1, 1))
                    + jnp.where(lane == 127, 0.0, pltpu.roll(after, 127, 1))
                )
                total[z + 2 - step, y + 2 - dy] += term

    @pl.when(step == 2)
    def _():
        for z in range(4):
            low_ref[z] = total[z, 0]
            inner_ref[z, 0] = total[z, 1]
            inner_ref[z, 1] = total[z, 2]
            high_ref[z] = total[z, 3]


def convolve(half, own, other, weight):
    whole = lambda shape: pl.BlockSpec(shape, lambda i: (0,) * len(shape))
    return pl.pallas_call(
        conv_kernel,
        grid=(3,),
        in_specs=[
            SMEM,
            whole((16, 4, 32, 128)),
            whole((16, 4, 32, 128)),
            pl.BlockSpec((1, 576, 1024), lambda i: (i, 0, 0)),
        ],
        out_specs=[whole((4, 64, 128)), whole((4, 2, 64, 128)), whole((4, 64, 128))],
        out_shape=[
            jax.ShapeDtypeStruct((4, 64, 128), F32),
            jax.ShapeDtypeStruct((4, 2, 64, 128), F32),
            jax.ShapeDtypeStruct((4, 64, 128), F32),
        ],
        scratch_shapes=[pltpu.VMEM((16, 2, 32, 512), BF16), pltpu.VMEM((4, 4, 64, 128), F32)],
        name="conv",
    )(half, own, other, weight)


def edge_kernel(inner_ref, before_ref, after_ref, low_ref, high_ref):
    for ref, z in ((low_ref, 0), (high_ref, 3)):
        ref[0] = inner_ref[z, 0] + before_ref[z]
        ref[1] = inner_ref[z, 1] + after_ref[z]


def edges(inner, before, after):
    shape = jax.ShapeDtypeStruct((2, 64, 128), F32)
    return pl.pallas_call(
        edge_kernel, in_specs=[VMEM] * 3, out_specs=[VMEM] * 2, out_shape=[shape, shape], name="edges"
    )(inner, before, after)


def gate_kernel(slot_ref, inner_ref, before_ref, after_ref, under_ref, over_ref, out_ref, turned, packed):
    slot = slot_ref[0]
    group = lax.broadcasted_iota(jnp.int32, (128, 128), 0) // 32
    for z in range(2):
        for y in range(2):
            side = (before_ref, after_ref)[y]
            ends = (under_ref, over_ref)[z]
            conv_out = inner_ref[z + 1, y] + side[z + 1] + ends[y]
            gate, value = conv_out[:32], conv_out[32:]
            gated = gate / (1.0 + jnp.exp(-gate)) * value
            spread = jnp.where(group == slot, jnp.concatenate([gated] * 4, axis=0), 0.0)
            turned[...] = spread.T
            for i in range(4):
                packed[pl.ds(i * 4 + z * 2 + y, 32, stride=16), :] = turned[pl.ds(i, 32, stride=4), :]
    out_ref[...] = packed[...].reshape(32, 16, 128).astype(BF16)


def gate(slot, inner, before, after, under, over):
    return pl.pallas_call(
        gate_kernel,
        in_specs=[SMEM] + [VMEM] * 5,
        out_specs=VMEM,
        out_shape=jax.ShapeDtypeStruct((32, 16, 128), BF16),
        scratch_shapes=[pltpu.VMEM((128, 128), F32), pltpu.VMEM((512, 128), F32)],
        name="gate",
    )(slot, inner, before, after, under, over)


def project_kernel(parts_ref, proj_ref, out_ref, held):
    chunks = []
    for k in range(8):
        chunk = parts_ref[4 * k].astype(F32)
        for i in range(1, 4):
            chunk = chunk + parts_ref[4 * k + i].astype(F32)
        chunks.append(chunk.astype(BF16))
    held[...] = jnp.dot(
        jnp.concatenate(chunks, axis=1), proj_ref[...], preferred_element_type=F32
    )
    block = lax.broadcasted_iota(jnp.int32, (4, 128), 1) // 32
    for b1 in range(4):
        rows = [held[i * 4 : (i + 1) * 4, b1 * 128 : (b1 + 1) * 128] for i in range(4)]
        hz1, hy1 = b1 // 2, b1 % 2
        for b2 in range(4):
            hz2, hy2 = b2 // 2, b2 % 2
            merged = None
            for i in range(4):
                shift = ((i - b2) % 4) * 32
                moved = rows[i] if shift == 0 else pltpu.roll(rows[i], shift, 1)
                merged = moved if merged is None else jnp.where(block == i, moved, merged)
            for z in range(2):
                for y in range(2):
                    at = ((z * 2 + hz1) * 2 + hz2) * 8 + y * 4 + hy1 * 2 + hy2
                    out_ref[at : at + 1, :] = merged[z * 2 + y : z * 2 + y + 1, :]


def project(parts, proj_weight):
    return pl.pallas_call(
        project_kernel,
        in_specs=[VMEM] * 2,
        out_specs=VMEM,
        out_shape=jax.ShapeDtypeStruct((64, 128), F32),
        scratch_shapes=[pltpu.VMEM((16, 512), F32)],
        name="project",
    )(parts, proj_weight)


def lift_pair(low, high):
    n = len(low)
    even = [low[i] - 0.25 * (high[i - 1] + high[i]) for i in range(1, n)]
    odd = [high[i] + 0.5 * (even[i - 1] + even[i]) for i in range(1, n - 1)]
    result = []
    for i in range(n - 2):
        result += [even[i], odd[i]]
    return result + [even[n - 2]]


def two_levels(cells):
    middle = [lift_pair([c[0][b] for c in cells], [c[1][b] for c in cells])[1:] for b in range(2)]
    return lift_pair(middle[0], middle[1])[:8]


def rows_of(ref, cell):
    return [[ref[pl.ds(((cell * 2 + h1) * 2 + h2) * 8, 8), :] for h2 in range(2)] for h1 in range(2)]


def extended_rows(own_ref, before_ref, after_ref):
    return [
        rows_of(before_ref, 0),
        rows_of(before_ref, 1),
        rows_of(own_ref, 0),
        rows_of(own_ref, 1),
        rows_of(after_ref, 0),
    ]


def lift_kernel(own_ref, before_ref, after_ref, out_ref):
    for i, fine in enumerate(two_levels(extended_rows(own_ref, before_ref, after_ref))):
        out_ref[pl.ds(i, 8, stride=8), :] = fine


def lift(own, before, after):
    return pl.pallas_call(
        lift_kernel,
        in_specs=[VMEM] * 3,
        out_specs=VMEM,
        out_shape=jax.ShapeDtypeStruct((64, 128), F32),
        name="lift",
    )(own, before, after)


def from_neighbours(to_next, to_previous, axis, closed):
    count = lax.axis_size(axis)
    ends = count if closed else count - 1
    before = lax.ppermute(to_next, axis, [(i, (i + 1) % count) for i in range(ends)])
    after = lax.ppermute(to_previous, axis, [((i + 1) % count, i) for i in range(ends)])
    return before, after


def on_device(volume, conv_weight, proj_weight):
    half = lax.axis_index("half")
    slot = (lax.axis_index("ring") * 2 + half) % 4
    own = lax.all_gather(volume.reshape(4, 32, 128), "ring", axis=0, tiled=False)
    other = lax.ppermute(own, "half", [(0, 1), (1, 0)])
    low, inner, high = convolve(
        half.reshape(1), own, other, conv_weight.reshape(3, 576, 1024)
    )
    before, after = from_neighbours(high, low, "gy", False)
    bottom, top = edges(inner, before, after)
    under, over = from_neighbours(top, bottom, "gz", False)
    sent = gate(slot.reshape(1), inner, before, after, under, over)
    parts = lax.all_to_all(sent, ("ring", "half"), split_axis=0, concat_axis=0, tiled=True)
    coefficients = project(parts, proj_weight)
    tall = lift(coefficients, *from_neighbours(coefficients, coefficients, "gz", True))
    fine = lift(tall, *from_neighbours(tall, tall, "gy", True))
    return fine.reshape(8, 8, 128)


def solution(mesh):
    split = Mesh(mesh.devices.reshape(4, 4, 16, 2), ("gz", "gy", "ring", "half"))
    col = ("ring", "half")
    return jax.shard_map(
        on_device,
        mesh=split,
        in_specs=(P("gz", "gy", col, None), P(None, None, col, None), P()),
        out_specs=P("gz", "gy", col),
        check_vma=False,
    )
```

time: 310 us -> 131 us (0.42)
  waiting for transfers between devices: 175 us -> 20.2 us
  blocking collectives: 21 us -> 57.5 us
  local copies, waits for them, and re-layouts: 35.8 us -> 3.31 us
  starting transfers between devices: 50.9 us -> 34.3 us
  Pallas kernels: 0 us -> 14.5 us
  between operations: 13.8 us -> 0.14 us
  matrix products: 9.42 us -> 0 us
  other arithmetic: 3.83 us -> 0 us
    all_gather x1 -> x0, waiting for transfers between devices: 159 us -> none  [on_device(): lax.all_gather(with_faces, 'col', axis=2, tiled=True)]
    all_gather x0 -> x1, blocking collectives: none -> 32 us  [on_device(): lax.all_gather(volume.reshape(4, 32, 128), 'ring', axis=0, tiled=False)]
    ppermute x12 -> x9, starting transfers between devices: 50.9 us -> 34.3 us  [the longest x4 21.7 us: from_neighbours(): lax.ppermute(to_next, axis, [(i, (i + 1) % count) for i in range(ends)])]
    pallas_call x0 -> x6, Pallas kernels: none -> 14.5 us  [the longest x1 5.71 us: convolve(): pl.pallas_call(conv_kernel, grid=(3,), in_specs=[SMEM, whole((16, 4, 32,...]
    unnamed x10 -> x20, local copies, waits for them, and re-layouts: 13.6 us -> 3.31 us
    conv_general_dilated x1 -> x0, matrix products: 7.92 us -> none  [convolve(): lax.conv_general_dilated(brick_data[None], kernel, (1, 1, 1), ((0, 0), (0...]
    slice x8 -> x0, local copies, waits for them, and re-layouts: 5.06 us -> none  [the longest x2 4.15 us: window_of(): return lax.slice_in_dim(array, first, last, axis=along)]
    ppermute x12 -> x9, waiting for transfers between devices: 15.4 us -> 20.2 us  [the longest x4 7.85 us: from_neighbours(): lax.ppermute(to_previous, axis, [((i + 1) % count, i) for i in range(ends)])]
  transfers between devices with their start and end apart: 13 -> 9, of which waited for: 7 -> 7; matrix products, arithmetic and copies ran while one was open for 0% -> 0% of each run, Pallas kernels for 0% -> 0%
where the time goes in v1:
time: 131 us; the launch traced here: 130 us
  blocking collectives  57.5 us (44%)
  starting transfers between devices  34.3 us (26%)
  waiting for transfers between devices  20.2 us (15%)
  Pallas kernels  14.5 us (11%)
  local copies, waits for them, and re-layouts  3.31 us (3%)
    all_gather x1, blocking collectives, on_device(): lax.all_gather(volume.reshape(4, 32, 128), 'ring', axis=0, tiled=False)  32 us
    all_to_all x1, blocking collectives, on_device(): lax.all_to_all(sent, ('ring', 'half'), split_axis=0, concat_axis=0, tiled...  25.5 us
    ppermute x4, starting transfers between devices, from_neighbours(): lax.ppermute(to_next, axis, [(i, (i + 1) % count) for i in range(ends)])  21.7 us
    ppermute x4, starting transfers between devices, from_neighbours(): lax.ppermute(to_previous, axis, [((i + 1) % count, i) for i in range(ends)])  7.97 us
    ppermute x4, waiting for transfers between devices, from_neighbours(): lax.ppermute(to_previous, axis, [((i + 1) % count, i) for i in range(ends)])  7.85 us
    ppermute x1, waiting for transfers between devices, on_device(): other = lax.ppermute(own, 'half', [(0, 1), (1, 0)])  6.77 us
    pallas_call x1, Pallas kernels, convolve(): pl.pallas_call(conv_kernel, grid=(3,), in_specs=[SMEM, whole((16, 4, 32,...  5.71 us
    ppermute x4, waiting for transfers between devices, from_neighbours(): lax.ppermute(to_next, axis, [(i, (i + 1) % count) for i in range(ends)])  5.55 us
  transfers between devices with their start and end apart: 9, of which 7 were waited for; matrix products, arithmetic and copies ran while one was open for 0% of the time, Pallas kernels for 0%

profile of v1, /device:TPU:1, one launch (start us, length us, event | category | flops | bytes accessed | tf_op | source)
XLA Modules:
  0.0 129.9 jit_solution(10747049821766384446)
XLA Ops:
  0.0 32.0 %all_gather.3.own_ref = bf16[16,4,32,128]{3,2,1,0:T(8,128)(2,1)S(1)} all-gather(bf16[1,4,32,128]{3,2,1,0:T(8,128)(2,1)} %bitcast.6), channel_id=1, replica_groups=mesh['gz'=4,'gy'=4,'ring'=16,'half'=2] {'ring'}, dimensions={0}, use_global_device_ids=true | all-gather | bytes 557056 | tf_op jit(solution)/shard_map/all_gather | solution.py:211
  32.0 4.6 %collective-permute-start = (bf16[16,4,32,128]{3,2,1,0:T(8,128)(2,1)S(1)}, bf16[16,4,32,128]{3,2,1,0:T(8,128)(2,1)S(1)}, u32[]{:S(2)}, u32[]{:S(2)}) collective-permute-start(bf16[16,4,32,128]{3,2,1,0:T(8,128)(2,1)S(1)} %all_gather.3.own_ref), channel_id=1, source_target_pairs={{0,1},{1,0},{2,3},{3,2},{4,5},{5,4},{6,7},{7,6},{8,9},{9,8},{10,11... | collective-permute-start | bytes 1572872 | tf_op jit(solution)/shard_map/ppermute | solution.py:212
  36.7 6.8 %collective-permute-done.other_ref = bf16[16,4,32,128]{3,2,1,0:T(8,128)(2,1)S(1)} collective-permute-done((bf16[16,4,32,128]{3,2,1,0:T(8,128)(2,1)S(1)}, bf16[16,4,32,128]{3,2,1,0:T(8,128)(2,1)S(1)}, u32[]{:S(2)}, u32[]{:S(2)}) %collective-permute-start) | collective-permute-done | bytes 524320 | tf_op jit(solution)/shard_map/ppermute | solution.py:212
  43.5 0.8 copy-done.1
  44.3 5.7 %conv.1 = (f32[4,64,128]{2,1,0:T(8,128)}, f32[4,2,64,128]{3,2,1,0:T(8,128)}, f32[4,64,128]{2,1,0:T(8,128)}) custom-call(s32[1]{0:T(128)} %bitcast.1.half_ref, bf16[16,4,32,128]{3,2,1,0:T(8,128)(2,1)} %copy-done, bf16[16,4,32,128]{3,2,1,0:T(8,128)(2,1)} %copy-done.1, bf16[3,576,1024]{2,1,0:T(8,128)(2,1)} %bitcast.5), custom_call_target="tpu_custom_call" | custom-call | tf_op jit(solution)/shard_map/conv/pallas_call | solution.py:57
  50.0 12.4 %collective-permute-start.1 = (f32[4,64,128]{2,1,0:T(8,128)}, f32[4,64,128]{2,1,0:T(8,128)S(1)}, u32[]{:S(2)}, u32[]{:S(2)}) collective-permute-start(f32[4,64,128]{2,1,0:T(8,128)} %get-tuple-element.11), channel_id=1, source_target_pairs={{0,32},{32,64},{64,96},{1,33},{33,65},{65,97},{2,34},{34,66},{66,9... | collective-permute-start | bytes 393224 | tf_op jit(solution)/shard_map/ppermute | solution.py:203
  62.4 1.9 %collective-permute-start.2 = (f32[4,64,128]{2,1,0:T(8,128)}, f32[4,64,128]{2,1,0:T(8,128)S(1)}, u32[]{:S(2)}, u32[]{:S(2)}) collective-permute-start(f32[4,64,128]{2,1,0:T(8,128)} %get-tuple-element.12), channel_id=1, source_target_pairs={{32,0},{64,32},{96,64},{33,1},{65,33},{97,65},{34,2},{66,34},{98,6... | collective-permute-start | bytes 393224 | tf_op jit(solution)/shard_map/ppermute | solution.py:204
  64.6 4.3 %collective-permute-done.2.after_ref = f32[4,64,128]{2,1,0:T(8,128)S(1)} collective-permute-done((f32[4,64,128]{2,1,0:T(8,128)}, f32[4,64,128]{2,1,0:T(8,128)S(1)}, u32[]{:S(2)}, u32[]{:S(2)}) %collective-permute-start.2) | collective-permute-done | bytes 131104 | tf_op jit(solution)/shard_map/ppermute | solution.py:204
  68.9 0.7 copy-done.3
  69.5 1.7 %edges.1 = (f32[2,64,128]{2,1,0:T(8,128)}, f32[2,64,128]{2,1,0:T(8,128)}) custom-call(f32[4,2,64,128]{3,2,1,0:T(8,128)} %get-tuple-element.10.inner_ref, f32[4,64,128]{2,1,0:T(8,128)} %copy-done.2, f32[4,64,128]{2,1,0:T(8,128)} %copy-done.3), custom_call_target="tpu_custom_call" | custom-call | tf_op jit(solution)/shard_map/edges/pallas_call | solution.py:85
  71.2 3.2 %collective-permute-start.3 = (f32[2,64,128]{2,1,0:T(8,128)}, f32[2,64,128]{2,1,0:T(8,128)S(1)}, u32[]{:S(2)}, u32[]{:S(2)}) collective-permute-start(f32[2,64,128]{2,1,0:T(8,128)} %get-tuple-element.13), channel_id=1, source_target_pairs={{0,128},{128,256},{256,384},{1,129},{129,257},{257,385},{2,130},{1... | collective-permute-start | bytes 196616 | tf_op jit(solution)/shard_map/ppermute | solution.py:203
  74.4 1.3 collective-permute-start.4
  76.1 3.6 %collective-permute-done.4.over_ref = f32[2,64,128]{2,1,0:T(8,128)S(1)} collective-permute-done((f32[2,64,128]{2,1,0:T(8,128)}, f32[2,64,128]{2,1,0:T(8,128)S(1)}, u32[]{:S(2)}, u32[]{:S(2)}) %collective-permute-start.4) | collective-permute-done | bytes 65568 | tf_op jit(solution)/shard_map/ppermute | solution.py:204
  80.3 2.0 %gate.1 = bf16[32,16,128]{2,1,0:T(8,128)(2,1)} custom-call(s32[1]{0:T(128)} %bitcast.slot_ref, f32[4,2,64,128]{3,2,1,0:T(8,128)} %get-tuple-element.10.inner_ref, f32[4,64,128]{2,1,0:T(8,128)} %copy-done.2, f32[4,64,128]{2,1,0:T(8,128)} %copy-done.3, f32[2,64,128]{2,1,0:T(8,128)} %copy-done.4, f32[2,64,128]{2,1,0:T(8,128)} %copy-done.5), custom_call_target="tpu_custom_call" | custom-call | tf_op jit(solution)/shard_map/gate/pallas_call | solution.py:108
  82.2 25.5 %all_to_all.5.parts_ref = bf16[32,16,128]{2,1,0:T(8,128)(2,1)} all-to-all(bf16[32,16,128]{2,1,0:T(8,128)(2,1)} %gate.1), channel_id=1, replica_groups=mesh['gz'=4,'gy'=4,'ring'=16,'half'=2] {'ring','half'}, dimensions={0} | all-to-all | bytes 262144 | tf_op jit(solution)/shard_map/all_to_all | solution.py:220
  107.7 2.3 %project.1.own_ref = f32[64,128]{1,0:T(8,128)} custom-call(bf16[32,16,128]{2,1,0:T(8,128)(2,1)} %all_to_all.5.parts_ref, bf16[1024,512]{1,0:T(8,128)(2,1)} %proj_ref.1), custom_call_target="tpu_custom_call" | custom-call | tf_op jit(solution)/shard_map/project/pallas_call | solution.py:146
  110.0 2.8 %collective-permute-start.6 = (f32[64,128]{1,0:T(8,128)}, f32[64,128]{1,0:T(8,128)S(1)}, u32[]{:S(2)}, u32[]{:S(2)}) collective-permute-start(f32[64,128]{1,0:T(8,128)} %project.1.own_ref), channel_id=1, source_target_pairs={{128,0},{256,128},{384,256},{0,384},{129,1},{257,129},{385,257},{1... | collective-permute-start | bytes 98312 | tf_op jit(solution)/shard_map/ppermute | solution.py:204
  112.8 2.4 %collective-permute-start.5 = (f32[64,128]{1,0:T(8,128)}, f32[64,128]{1,0:T(8,128)S(1)}, u32[]{:S(2)}, u32[]{:S(2)}) collective-permute-start(f32[64,128]{1,0:T(8,128)} %project.1.own_ref), channel_id=1, source_target_pairs={{0,128},{128,256},{256,384},{384,0},{1,129},{129,257},{257,385},{3... | collective-permute-start | bytes 98312 | tf_op jit(solution)/shard_map/ppermute | solution.py:203
  115.3 3.6 %collective-permute-done.5.before_ref = f32[64,128]{1,0:T(8,128)S(1)} collective-permute-done((f32[64,128]{1,0:T(8,128)}, f32[64,128]{1,0:T(8,128)S(1)}, u32[]{:S(2)}, u32[]{:S(2)}) %collective-permute-start.5) | collective-permute-done | bytes 32800 | tf_op jit(solution)/shard_map/ppermute | solution.py:203
  119.5 1.4 %lift.2.own_ref = f32[64,128]{1,0:T(8,128)} custom-call(f32[64,128]{1,0:T(8,128)} %project.1.own_ref, f32[64,128]{1,0:T(8,128)} %copy-done.8, f32[64,128]{1,0:T(8,128)} %copy-done.6), custom_call_target="tpu_custom_call" | custom-call | tf_op jit(solution)/shard_map/lift/pallas_call | solution.py:191
  120.9 1.9 %collective-permute-start.8 = (f32[64,128]{1,0:T(8,128)}, f32[64,128]{1,0:T(8,128)S(1)}, u32[]{:S(2)}, u32[]{:S(2)}) collective-permute-start(f32[64,128]{1,0:T(8,128)} %lift.2.own_ref), channel_id=1, source_target_pairs={{32,0},{64,32},{96,64},{0,96},{33,1},{65,33},{97,65},{1,97},{34,2}... | collective-permute-start | bytes 98312 | tf_op jit(solution)/shard_map/ppermute | solution.py:204
  122.9 3.7 %collective-permute-start.7 = (f32[64,128]{1,0:T(8,128)}, f32[64,128]{1,0:T(8,128)S(1)}, u32[]{:S(2)}, u32[]{:S(2)}) collective-permute-start(f32[64,128]{1,0:T(8,128)} %lift.2.own_ref), channel_id=1, source_target_pairs={{0,32},{32,64},{64,96},{96,0},{1,33},{33,65},{65,97},{97,1},{2,34}... | collective-permute-start | bytes 98312 | tf_op jit(solution)/shard_map/ppermute | solution.py:203
  126.5 1.3 collective-permute-done.7.before_ref
  128.5 1.4 %lift.3 = f32[64,128]{1,0:T(8,128)} custom-call(f32[64,128]{1,0:T(8,128)} %lift.2.own_ref, f32[64,128]{1,0:T(8,128)} %copy-done.9, f32[64,128]{1,0:T(8,128)} %copy-done.7), custom_call_target="tpu_custom_call" | custom-call | tf_op jit(solution)/shard_map/lift/pallas_call | solution.py:191
  (22 shorter events, 2.5 us)
Async XLA Ops:
  32.0 11.4 %copy-start = (bf16[16,4,32,128]{3,2,1,0:T(8,128)(2,1)}, bf16[16,4,32,128]{3,2,1,0:T(8,128)(2,1)S(1)}, u32[]{:S(2)}) copy-start(bf16[16,4,32,128]{3,2,1,0:T(8,128)(2,1)S(1)} %all_gather.3.own_ref) | copy-start | bytes 1572868
  32.0 11.4 %collective-permute-start = (bf16[16,4,32,128]{3,2,1,0:T(8,128)(2,1)S(1)}, bf16[16,4,32,128]{3,2,1,0:T(8,128)(2,1)S(1)}, u32[]{:S(2)}, u32[]{:S(2)}) collective-permute-start(bf16[16,4,32,128]{3,2,1,0:T(8,128)(2,1)S(1)} %all_gather.3.own_ref), channel_id=1, source_target_pairs={{0,1},{1,0},{2,3},{3,2},{4,5},{5,4},{6,7},{7,6},{8,9},{9,8},{10,11... | collective-permute-start | bytes 1572872 | tf_op jit(solution)/shard_map/ppermute | solution.py:212
  43.5 0.8 copy-start.1
  50.0 14.6 %collective-permute-start.1 = (f32[4,64,128]{2,1,0:T(8,128)}, f32[4,64,128]{2,1,0:T(8,128)S(1)}, u32[]{:S(2)}, u32[]{:S(2)}) collective-permute-start(f32[4,64,128]{2,1,0:T(8,128)} %get-tuple-element.11), channel_id=1, source_target_pairs={{0,32},{32,64},{64,96},{1,33},{33,65},{65,97},{2,34},{34,66},{66,9... | collective-permute-start | bytes 393224 | tf_op jit(solution)/shard_map/ppermute | solution.py:203
  62.4 6.5 %collective-permute-start.2 = (f32[4,64,128]{2,1,0:T(8,128)}, f32[4,64,128]{2,1,0:T(8,128)S(1)}, u32[]{:S(2)}, u32[]{:S(2)}) collective-permute-start(f32[4,64,128]{2,1,0:T(8,128)} %get-tuple-element.12), channel_id=1, source_target_pairs={{32,0},{64,32},{96,64},{33,1},{65,33},{97,65},{34,2},{66,34},{98,6... | collective-permute-start | bytes 393224 | tf_op jit(solution)/shard_map/ppermute | solution.py:204
  64.6 4.3 %copy-start.2 = (f32[4,64,128]{2,1,0:T(8,128)}, f32[4,64,128]{2,1,0:T(8,128)S(1)}, u32[]{:S(2)}) copy-start(f32[4,64,128]{2,1,0:T(8,128)S(1)} %collective-permute-done.1.before_ref) | copy-start | bytes 393220
  68.9 0.7 copy-start.3
  71.2 4.8 %collective-permute-start.3 = (f32[2,64,128]{2,1,0:T(8,128)}, f32[2,64,128]{2,1,0:T(8,128)S(1)}, u32[]{:S(2)}, u32[]{:S(2)}) collective-permute-start(f32[2,64,128]{2,1,0:T(8,128)} %get-tuple-element.13), channel_id=1, source_target_pairs={{0,128},{128,256},{256,384},{1,129},{129,257},{257,385},{2,130},{1... | collective-permute-start | bytes 196616 | tf_op jit(solution)/shard_map/ppermute | solution.py:203
  74.4 5.2 %collective-permute-start.4 = (f32[2,64,128]{2,1,0:T(8,128)}, f32[2,64,128]{2,1,0:T(8,128)S(1)}, u32[]{:S(2)}, u32[]{:S(2)}) collective-permute-start(f32[2,64,128]{2,1,0:T(8,128)} %get-tuple-element.14), channel_id=1, source_target_pairs={{128,0},{256,128},{384,256},{129,1},{257,129},{385,257},{130,2},{2... | collective-permute-start | bytes 196616 | tf_op jit(solution)/shard_map/ppermute | solution.py:204
  76.1 3.6 %copy-start.4 = (f32[2,64,128]{2,1,0:T(8,128)}, f32[2,64,128]{2,1,0:T(8,128)S(1)}, u32[]{:S(2)}) copy-start(f32[2,64,128]{2,1,0:T(8,128)S(1)} %collective-permute-done.3.under_ref) | copy-start | bytes 196612
  79.6 0.6 copy-start.5
  110.0 5.3 %collective-permute-start.6 = (f32[64,128]{1,0:T(8,128)}, f32[64,128]{1,0:T(8,128)S(1)}, u32[]{:S(2)}, u32[]{:S(2)}) collective-permute-start(f32[64,128]{1,0:T(8,128)} %project.1.own_ref), channel_id=1, source_target_pairs={{128,0},{256,128},{384,256},{0,384},{129,1},{257,129},{385,257},{1... | collective-permute-start | bytes 98312 | tf_op jit(solution)/shard_map/ppermute | solution.py:204
  112.8 6.1 %collective-permute-start.5 = (f32[64,128]{1,0:T(8,128)}, f32[64,128]{1,0:T(8,128)S(1)}, u32[]{:S(2)}, u32[]{:S(2)}) collective-permute-start(f32[64,128]{1,0:T(8,128)} %project.1.own_ref), channel_id=1, source_target_pairs={{0,128},{128,256},{256,384},{384,0},{1,129},{129,257},{257,385},{3... | collective-permute-start | bytes 98312 | tf_op jit(solution)/shard_map/ppermute | solution.py:203
  115.3 3.6 %copy-start.6 = (f32[64,128]{1,0:T(8,128)}, f32[64,128]{1,0:T(8,128)S(1)}, u32[]{:S(2)}) copy-start(f32[64,128]{1,0:T(8,128)S(1)} %collective-permute-done.6.after_ref) | copy-start | bytes 98308
  118.9 0.6 copy-start.8
  120.9 5.6 %collective-permute-start.8 = (f32[64,128]{1,0:T(8,128)}, f32[64,128]{1,0:T(8,128)S(1)}, u32[]{:S(2)}, u32[]{:S(2)}) collective-permute-start(f32[64,128]{1,0:T(8,128)} %lift.2.own_ref), channel_id=1, source_target_pairs={{32,0},{64,32},{96,64},{0,96},{33,1},{65,33},{97,65},{1,97},{34,2}... | collective-permute-start | bytes 98312 | tf_op jit(solution)/shard_map/ppermute | solution.py:204
  122.9 5.0 %collective-permute-start.7 = (f32[64,128]{1,0:T(8,128)}, f32[64,128]{1,0:T(8,128)S(1)}, u32[]{:S(2)}, u32[]{:S(2)}) collective-permute-start(f32[64,128]{1,0:T(8,128)} %lift.2.own_ref), channel_id=1, source_target_pairs={{0,32},{32,64},{64,96},{96,0},{1,33},{33,65},{65,97},{97,1},{2,34}... | collective-permute-start | bytes 98312 | tf_op jit(solution)/shard_map/ppermute | solution.py:203
  126.5 1.3 %copy-start.7 = (f32[64,128]{1,0:T(8,128)}, f32[64,128]{1,0:T(8,128)S(1)}, u32[]{:S(2)}) copy-start(f32[64,128]{1,0:T(8,128)S(1)} %collective-permute-done.8.after_ref) | copy-start | bytes 98308
  127.8 0.6 copy-start.9

commit v2 on v1

v2 whole, which is shorter than its diff:
```python
import jax
import jax.numpy as jnp
from jax import lax
from jax.experimental import pallas as pl
from jax.experimental.pallas import tpu as pltpu
from jax.sharding import Mesh, PartitionSpec as P

F32 = jnp.float32
BF16 = jnp.bfloat16
VMEM = pl.BlockSpec(memory_space=pltpu.VMEM)
SMEM = pl.BlockSpec(memory_space=pltpu.SMEM)


def conv_kernel(half_ref, own_ref, other_ref, weight_ref, keep_ref, y_ref, z_ref, corner_ref, cells, total):
    step = pl.program_id(0)

    @pl.when(step == 0)
    def _():
        half = half_ref[0]
        for k in range(16):
            for row in range(4):
                lanes = pl.ds(row * 128, 128)
                cells[k, half, :, lanes] = own_ref[k, row]
                cells[k, 1 - half, :, lanes] = other_ref[k, row]
        total[...] = jnp.zeros_like(total)

    products = jnp.dot(
        weight_ref[0], cells[...].reshape(1024, 512), preferred_element_type=F32
    )
    lane = lax.broadcasted_iota(jnp.int32, (64, 128), 1)
    for dy in range(3):
        for z in range(2):
            for y in range(2):
                row = z * 2 + y
                before, centre, after = (
                    products[(dy * 3 + dx) * 64 : (dy * 3 + dx + 1) * 64, row * 128 : (row + 1) * 128]
                    for dx in range(3)
                )
                term = (
                    centre
                    + jnp.where(lane == 0, 0.0, pltpu.roll(before, 1, 1))
                    + jnp.where(lane == 127, 0.0, pltpu.roll(after, 127, 1))
                )
                total[z + 2 - step, y + 2 - dy] += term

    @pl.when(step == 2)
    def _():
        for ref, top, left in ((keep_ref, 0, 0), (y_ref, 0, 2), (z_ref, 2, 0), (corner_ref, 2, 2)):
            for z in range(2):
                for y in range(2):
                    ref[z, y] = total[top + z, left + y]


def convolve(half, own, other, weight):
    whole = lambda shape: pl.BlockSpec(shape, lambda i: (0,) * len(shape))
    return pl.pallas_call(
        conv_kernel,
        grid=(3,),
        in_specs=[SMEM, VMEM, VMEM, pl.BlockSpec((1, 576, 1024), lambda i: (i, 0, 0))],
        out_specs=[whole((2, 2, 64, 128))] * 4,
        out_shape=[jax.ShapeDtypeStruct((2, 2, 64, 128), F32)] * 4,
        scratch_shapes=[pltpu.VMEM((16, 2, 32, 512), BF16), pltpu.VMEM((4, 4, 64, 128), F32)],
        compiler_params=pltpu.CompilerParams(vmem_limit_bytes=16 << 20),
        name="conv",
    )(half, own, other, weight)


def gate_kernel(slot_ref, gz_ref, gy_ref, keep_ref, y_ref, z_ref, corner_ref, out_ref, turned, packed):
    slot = slot_ref[0]
    inside = [jnp.where(ref[0] > 0, 1.0, 0.0) for ref in (gz_ref, gy_ref)]
    group = lax.broadcasted_iota(jnp.int32, (128, 128), 0) // 32
    for z in range(2):
        for y in range(2):
            z_own, z_before = ((inside[0], 1.0), (1.0, inside[0]))[z]
            y_own, y_before = ((inside[1], 1.0), (1.0, inside[1]))[y]
            conv_out = (
                keep_ref[z, y] * (z_own * y_own)
                + y_ref[z, y] * (z_own * y_before)
                + z_ref[z, y] * (z_before * y_own)
                + corner_ref[z, y] * (z_before * y_before)
            )
            gate, value = conv_out[:32], conv_out[32:]
            gated = gate / (1.0 + jnp.exp(-gate)) * value
            spread = jnp.where(group == slot, jnp.concatenate([gated] * 4, axis=0), 0.0)
            turned[...] = spread.T
            for i in range(4):
                packed[pl.ds(i * 4 + z * 2 + y, 32, stride=16), :] = turned[pl.ds(i, 32, stride=4), :]
    out_ref[...] = packed[...].reshape(32, 16, 128).astype(BF16)


def gate(slot, gz, gy, *pieces):
    return pl.pallas_call(
        gate_kernel,
        in_specs=[SMEM] * 3 + [VMEM] * 4,
        out_specs=VMEM,
        out_shape=jax.ShapeDtypeStruct((32, 16, 128), BF16),
        scratch_shapes=[pltpu.VMEM((128, 128), F32), pltpu.VMEM((512, 128), F32)],
        compiler_params=pltpu.CompilerParams(vmem_limit_bytes=4 << 20),
        name="gate",
    )(slot, gz, gy, *pieces)


S, D = (0, 1), (2, 3)


def to_previous(slots):
    even = [slots[4 + S[h]] - 0.25 * (slots[D[h]] + slots[4 + D[h]]) for h in range(2)]
    return slots[:4] + even


def to_next(slots):
    return [slots[4 + D[h]] for h in range(2)]


def project_kernel(gz_ref, gy_ref, parts_ref, proj_ref, own_ref, sent_ref, held, turned):
    chunks = []
    for k in range(8):
        chunk = parts_ref[4 * k].astype(F32)
        for i in range(1, 4):
            chunk = chunk + parts_ref[4 * k + i].astype(F32)
        chunks.append(chunk.astype(BF16))
    held[...] = jnp.dot(
        jnp.concatenate(chunks, axis=1), proj_ref[...], preferred_element_type=F32
    )
    block = lax.broadcasted_iota(jnp.int32, (4, 128), 1) // 32
    for b1 in range(4):
        rows = [held[i * 4 : (i + 1) * 4, b1 * 128 : (b1 + 1) * 128] for i in range(4)]
        hz1, hy1 = b1 // 2, b1 % 2
        for b2 in range(4):
            hz2, hy2 = b2 // 2, b2 % 2
            merged = None
            for i in range(4):
                shift = ((i - b2) % 4) * 32
                moved = rows[i] if shift == 0 else pltpu.roll(rows[i], shift, 1)
                merged = moved if merged is None else jnp.where(block == i, moved, merged)
            for z in range(2):
                for y in range(2):
                    row = merged[z * 2 + y : z * 2 + y + 1, :]
                    z_slot, y_slot = z * 4 + hz1 * 2 + hz2, y * 4 + hy1 * 2 + hy2
                    own_ref[z_slot, y_slot : y_slot + 1, :] = row
                    turned[y_slot, z_slot : z_slot + 1, :] = row

    gz, gy = gz_ref[0], gy_ref[0]
    sent_ref[...] = jnp.zeros_like(sent_ref)

    def send(dz, dy, slots):
        at = ((gz + dz) % 4) * 4 + (gy + dy) % 4
        for k, slot in enumerate(slots):
            sent_ref[at, k] = slot

    by_z = [own_ref[k] for k in range(8)]
    by_y = [turned[k] for k in range(8)]
    for dy in (3, 0, 1):
        send(3, dy, to_previous(by_z))
        send(1, dy, to_next(by_z))
    send(0, 3, to_previous(by_y))
    send(0, 1, to_next(by_y))


def project(gz, gy, parts, proj_weight):
    return pl.pallas_call(
        project_kernel,
        in_specs=[SMEM] * 2 + [VMEM] * 2,
        out_specs=[VMEM] * 2,
        out_shape=[
            jax.ShapeDtypeStruct((8, 8, 128), F32),
            jax.ShapeDtypeStruct((16, 6, 8, 128), F32),
        ],
        scratch_shapes=[pltpu.VMEM((16, 512), F32), pltpu.VMEM((8, 8, 128), F32)],
        compiler_params=pltpu.CompilerParams(vmem_limit_bytes=8 << 20),
        name="project",
    )(gz, gy, parts, proj_weight)


def lift_pair(low, high):
    n = len(low)
    even = [low[i] - 0.25 * (high[i - 1] + high[i]) for i in range(1, n)]
    odd = [high[i] + 0.5 * (even[i - 1] + even[i]) for i in range(1, n - 1)]
    result = []
    for i in range(n - 2):
        result += [even[i], odd[i]]
    return result + [even[n - 2]]


def two_levels(before, own, after):
    middle = []
    for h in range(2):
        low = [own[S[h]], own[4 + S[h]], after[S[h]]]
        high = [before[h], own[D[h]], own[4 + D[h]], after[D[h]]]
        even = [low[i] - 0.25 * (high[i] + high[i + 1]) for i in range(3)] + [after[4 + h]]
        odd = [high[i + 1] + 0.5 * (even[i] + even[i + 1]) for i in range(3)]
        middle.append([odd[0], even[1], odd[1], even[2], odd[2], even[3]])
    return lift_pair(middle[0], middle[1])[:8]


def lift_kernel(gz_ref, gy_ref, own_ref, got_ref, out_ref, across, tall):
    gz, gy = gz_ref[0], gy_ref[0]
    at = lambda dz, dy: ((gz + dz) % 4) * 4 + (gy + dy) % 4
    after, before = at(0, 1), at(0, 3)
    for k in range(6):
        across[1, :, k, :] = got_ref[after, k]
    for k in range(2):
        across[0, :, 6 + k, :] = got_ref[before, k]
    sub = lax.broadcasted_iota(jnp.int32, (8, 128), 0)

    def shortened(cells):
        even = cells - 0.25 * (pltpu.roll(cells, 2, 0) + pltpu.roll(cells, 6, 0))
        return jnp.where(sub < 4, cells, even)

    for side, dy in ((0, 3), (1, 1), (2, 0)):
        change = shortened if side == 1 else lambda cells: cells
        below = [change(got_ref[at(3, dy), k]) for k in range(2)]
        above = [change(got_ref[at(1, dy), k]) for k in range(6)]
        centre = [own_ref[k] if side == 2 else across[side, k] for k in range(8)]
        for i, fine in enumerate(two_levels(below, centre, above)):
            tall[side, :, i, :] = fine
    fine = two_levels(
        [tall[0, 6 + k] for k in range(2)],
        [tall[2, k] for k in range(8)],
        [tall[1, k] for k in range(6)],
    )
    for i in range(8):
        out_ref[:, i, :] = fine[i]


def lift(gz, gy, own, got):
    return pl.pallas_call(
        lift_kernel,
        in_specs=[SMEM] * 2 + [VMEM] * 2,
        out_specs=VMEM,
        out_shape=jax.ShapeDtypeStruct((8, 8, 128), F32),
        scratch_shapes=[pltpu.VMEM((2, 8, 8, 128), F32), pltpu.VMEM((3, 8, 8, 128), F32)],
        compiler_params=pltpu.CompilerParams(vmem_limit_bytes=4 << 20),
        name="lift",
    )(gz, gy, own, got)


def on_device(volume, conv_weight, proj_weight):
    half = lax.axis_index("half")
    slot = ((lax.axis_index("ring") * 2 + half) % 4).reshape(1)
    gz, gy = (lax.axis_index(axis).reshape(1) for axis in ("gz", "gy"))
    own = lax.all_gather(volume.reshape(4, 32, 128), "ring", axis=0, tiled=False)
    other = lax.ppermute(own, "half", [(0, 1), (1, 0)])
    keep, to_y, to_z, to_corner = convolve(
        half.reshape(1), own, other, conv_weight.reshape(3, 576, 1024)
    )
    step = [(i, (i + 1) % 4) for i in range(4)]
    both = [(a * 4 + b, c * 4 + d) for a, c in step for b, d in step]
    sent = gate(
        slot,
        gz,
        gy,
        keep,
        lax.ppermute(to_y, "gy", step),
        lax.ppermute(to_z, "gz", step),
        lax.ppermute(to_corner, ("gz", "gy"), both),
    )
    parts = lax.all_to_all(sent, ("ring", "half"), split_axis=0, concat_axis=0, tiled=True)
    coefficients, messages = project(gz, gy, parts, proj_weight)
    got = lax.all_to_all(messages, ("gz", "gy"), split_axis=0, concat_axis=0, tiled=True)
    return lift(gz, gy, coefficients, got)


def solution(mesh):
    split = Mesh(mesh.devices.reshape(4, 4, 16, 2), ("gz", "gy", "ring", "half"))
    col = ("ring", "half")
    return jax.shard_map(
        on_device,
        mesh=split,
        in_specs=(P("gz", "gy", col, None), P(None, None, col, None), P()),
        out_specs=P("gz", "gy", col),
        check_vma=False,
    )
```

time: 131 us -> 111 us (0.85)
  blocking collectives: 57.5 us -> 69.1 us
  starting transfers between devices: 34.3 us -> 23.5 us
  Pallas kernels: 14.5 us -> 4.38 us
  waiting for transfers between devices: 20.2 us -> 11.8 us
  local copies, waits for them, and re-layouts: 3.31 us -> 2 us
    all_to_all x0 -> x1, blocking collectives: none -> 11.5 us  [on_device(): lax.all_to_all(messages, ('gz', 'gy'), split_axis=0, concat_axis=0, tiled...]
    ppermute x8 -> x3, starting transfers between devices: 29.6 us -> 18.8 us  [the longest x1 12.4 us: on_device(): lax.ppermute(to_y, 'gy', step)]
    pallas_call x6 -> x4, Pallas kernels: 14.5 us -> 4.38 us  [the longest x1 3 us: convolve(): pl.pallas_call(conv_kernel, grid=(3,), in_specs=[SMEM, VMEM, VMEM, pl.Blo...]
    ppermute x8 -> x3, waiting for transfers between devices: 13.4 us -> 5.07 us  [the longest x1 3.82 us: on_device(): lax.ppermute(to_corner, ('gz', 'gy'), both)]
    unnamed x20 -> x4, local copies, waits for them, and re-layouts: 3.31 us -> 2 us
  transfers between devices with their start and end apart: 9 -> 4, of which waited for: 7 -> 3; matrix products, arithmetic and copies ran while one was open for 0% -> 0% of each run, Pallas kernels for 0% -> 0%
where the time goes in v2:
time: 111 us
  blocking collectives  69.1 us (62%)
  starting transfers between devices  23.5 us (21%)
  waiting for transfers between devices  11.8 us (11%)
  Pallas kernels  4.38 us (4%)
  local copies, waits for them, and re-layouts  2 us (2%)
    all_gather x1, blocking collectives, on_device(): lax.all_gather(volume.reshape(4, 32, 128), 'ring', axis=0, tiled=False)  32 us
    all_to_all x1, blocking collectives, on_device(): lax.all_to_all(sent, ('ring', 'half'), split_axis=0, concat_axis=0, tiled...  25.6 us
    ppermute x1, starting transfers between devices, on_device(): lax.ppermute(to_y, 'gy', step)  12.4 us
    all_to_all x1, blocking collectives, on_device(): lax.all_to_all(messages, ('gz', 'gy'), split_axis=0, concat_axis=0, tiled...  11.5 us
    ppermute x1, waiting for transfers between devices, on_device(): other = lax.ppermute(own, 'half', [(0, 1), (1, 0)])  6.77 us
    ppermute x1, starting transfers between devices, on_device(): other = lax.ppermute(own, 'half', [(0, 1), (1, 0)])  4.64 us
    ppermute x1, waiting for transfers between devices, on_device(): lax.ppermute(to_corner, ('gz', 'gy'), both)  3.82 us
    ppermute x1, starting transfers between devices, on_device(): lax.ppermute(to_z, 'gz', step)  3.21 us
  transfers between devices with their start and end apart: 4, of which 3 were waited for; matrix products, arithmetic and copies ran while one was open for 0% of the time, Pallas kernels for 0%

profile of v2, /device:TPU:1, one launch (start us, length us, event | category | flops | bytes accessed | tf_op | source)
XLA Modules:
  0.0 110.8 jit_solution(14296324067616884747)
XLA Ops:
  0.0 32.0 %all_gather.3.own_ref = bf16[16,4,32,128]{3,2,1,0:T(8,128)(2,1)S(1)} all-gather(bf16[1,4,32,128]{3,2,1,0:T(8,128)(2,1)} %bitcast.7), channel_id=1, replica_groups=mesh['gz'=4,'gy'=4,'ring'=16,'half'=2] {'ring'}, dimensions={0}, use_global_device_ids=true | all-gather | bytes 557056 | tf_op jit(solution)/shard_map/all_gather | solution.py:242
  32.0 4.6 %collective-permute-start = (bf16[16,4,32,128]{3,2,1,0:T(8,128)(2,1)S(1)}, bf16[16,4,32,128]{3,2,1,0:T(8,128)(2,1)S(1)}, u32[]{:S(2)}, u32[]{:S(2)}) collective-permute-start(bf16[16,4,32,128]{3,2,1,0:T(8,128)(2,1)S(1)} %all_gather.3.own_ref), channel_id=1, source_target_pairs={{0,1},{1,0},{2,3},{3,2},{4,5},{5,4},{6,7},{7,6},{8,9},{9,8},{10,11... | collective-permute-start | bytes 1572872 | tf_op jit(solution)/shard_map/ppermute | solution.py:243
  36.7 6.8 %collective-permute-done.other_ref = bf16[16,4,32,128]{3,2,1,0:T(8,128)(2,1)S(1)} collective-permute-done((bf16[16,4,32,128]{3,2,1,0:T(8,128)(2,1)S(1)}, bf16[16,4,32,128]{3,2,1,0:T(8,128)(2,1)S(1)}, u32[]{:S(2)}, u32[]{:S(2)}) %collective-permute-start) | collective-permute-done | bytes 524320 | tf_op jit(solution)/shard_map/ppermute | solution.py:243
  43.5 0.0 copy-start
  43.5 2.0 %copy-done = bf16[27,2,32,1024]{3,2,1,0:T(8,128)(2,1)S(1)} copy-done((bf16[27,2,32,1024]{3,2,1,0:T(8,128)(2,1)S(1)}, bf16[27,2,32,1024]{3,2,1,0:T(8,128)(2,1)}, u32[]{:S(2)}) %copy-start) | copy-done | bytes 3538968
  45.5 0.0 copy-start.1
  45.5 3.0 %conv.1 = (f32[2,2,64,128]{3,2,1,0:T(8,128)S(1)}, f32[2,2,64,128]{3,2,1,0:T(8,128)S(1)}, f32[2,2,64,128]{3,2,1,0:T(8,128)S(1)}, f32[2,2,64,128]{3,2,1,0:T(8,128)S(1)}) custom-call(s32[1]{0:T(128)} %bitcast.3.half_ref, bf16[16,4,32,128]{3,2,1,0:T(8,128)(2,1)S(1)} %all_gather.3.own_ref, bf16[16,4,32,128]{3,2,1,0:T(8,128)(2,1)S(1)} %collective-permute-done.other_ref, ...), custom_call_target="tpu_custom_call" | custom-call | tf_op jit(solution)/shard_map/conv/pallas_call | solution.py:56
  48.5 12.4 %collective-permute-start.1 = (f32[2,2,64,128]{3,2,1,0:T(8,128)S(1)}, f32[2,2,64,128]{3,2,1,0:T(8,128)S(1)}, u32[]{:S(2)}, u32[]{:S(2)}) collective-permute-start(f32[2,2,64,128]{3,2,1,0:T(8,128)S(1)} %get-tuple-element.12), channel_id=1, source_target_pairs={{0,32},{32,64},{64,96},{96,0},{1,33},{33,65},{65,97},{97,1},{2,34}... | collective-permute-start | bytes 393224 | tf_op jit(solution)/shard_map/ppermute | solution.py:254
  60.9 3.2 %collective-permute-start.2 = (f32[2,2,64,128]{3,2,1,0:T(8,128)S(1)}, f32[2,2,64,128]{3,2,1,0:T(8,128)S(1)}, u32[]{:S(2)}, u32[]{:S(2)}) collective-permute-start(f32[2,2,64,128]{3,2,1,0:T(8,128)S(1)} %get-tuple-element.13), channel_id=1, source_target_pairs={{0,128},{128,256},{256,384},{384,0},{1,129},{129,257},{257,385},{3... | collective-permute-start | bytes 393224 | tf_op jit(solution)/shard_map/ppermute | solution.py:255
  64.1 3.2 %collective-permute-start.3 = (f32[2,2,64,128]{3,2,1,0:T(8,128)S(1)}, f32[2,2,64,128]{3,2,1,0:T(8,128)S(1)}, u32[]{:S(2)}, u32[]{:S(2)}) collective-permute-start(f32[2,2,64,128]{3,2,1,0:T(8,128)S(1)} %get-tuple-element.14), channel_id=1, source_target_pairs={{0,160},{32,192},{64,224},{96,128},{128,288},{160,320},{192,352},{... | collective-permute-start | bytes 393224 | tf_op jit(solution)/shard_map/ppermute | solution.py:256
  67.3 0.0 collective-permute-done.1.y_ref
  67.3 1.2 %collective-permute-done.2.z_ref = f32[2,2,64,128]{3,2,1,0:T(8,128)S(1)} collective-permute-done((f32[2,2,64,128]{3,2,1,0:T(8,128)S(1)}, f32[2,2,64,128]{3,2,1,0:T(8,128)S(1)}, u32[]{:S(2)}, u32[]{:S(2)}) %collective-permute-start.2) | collective-permute-done | bytes 131104 | tf_op jit(solution)/shard_map/ppermute | solution.py:255
  68.6 3.8 %collective-permute-done.3.corner_ref = f32[2,2,64,128]{3,2,1,0:T(8,128)S(1)} collective-permute-done((f32[2,2,64,128]{3,2,1,0:T(8,128)S(1)}, f32[2,2,64,128]{3,2,1,0:T(8,128)S(1)}, u32[]{:S(2)}, u32[]{:S(2)}) %collective-permute-start.3) | collective-permute-done | bytes 131104 | tf_op jit(solution)/shard_map/ppermute | solution.py:256
  72.4 0.2 gate.1
  72.6 25.6 %all_to_all.10.parts_ref = bf16[32,16,128]{2,1,0:T(8,128)(2,1)S(1)} all-to-all(bf16[32,16,128]{2,1,0:T(8,128)(2,1)S(1)} %gate.1), channel_id=1, replica_groups=mesh['gz'=4,'gy'=4,'ring'=16,'half'=2] {'ring','half'}, dimensions={0} | all-to-all | bytes 262144 | tf_op jit(solution)/shard_map/all_to_all | solution.py:258
  98.2 0.0 copy-done.1
  98.2 0.4 project.1
  98.6 11.5 %all_to_all.11.got_ref = f32[16,6,8,128]{3,2,1,0:T(8,128)S(1)} all-to-all(f32[16,6,8,128]{3,2,1,0:T(8,128)S(1)} %get-tuple-element.16), channel_id=1, replica_groups=mesh['gz'=4,'gy'=4,'ring'=16,'half'=2] {'gz','gy'}, dimensions={0} | all-to-all | bytes 786432 | tf_op jit(solution)/shard_map/all_to_all | solution.py:260
  110.1 0.7 lift.1
Async XLA Ops:
  32.0 11.4 %collective-permute-start = (bf16[16,4,32,128]{3,2,1,0:T(8,128)(2,1)S(1)}, bf16[16,4,32,128]{3,2,1,0:T(8,128)(2,1)S(1)}, u32[]{:S(2)}, u32[]{:S(2)}) collective-permute-start(bf16[16,4,32,128]{3,2,1,0:T(8,128)(2,1)S(1)} %all_gather.3.own_ref), channel_id=1, source_target_pairs={{0,1},{1,0},{2,3},{3,2},{4,5},{5,4},{6,7},{7,6},{8,9},{9,8},{10,11... | collective-permute-start | bytes 1572872 | tf_op jit(solution)/shard_map/ppermute | solution.py:243
  43.5 2.0 %copy-start = (bf16[27,2,32,1024]{3,2,1,0:T(8,128)(2,1)S(1)}, bf16[27,2,32,1024]{3,2,1,0:T(8,128)(2,1)}, u32[]{:S(2)}) copy-start(bf16[27,2,32,1024]{3,2,1,0:T(8,128)(2,1)} %param.4) | copy-start | bytes 10616836
  45.5 52.7 %copy-start.1 = (bf16[1024,512]{1,0:T(8,128)(2,1)S(1)}, bf16[1024,512]{1,0:T(8,128)(2,1)}, u32[]{:S(2)}) copy-start(bf16[1024,512]{1,0:T(8,128)(2,1)} %proj_ref.1) | copy-start | bytes 3145732
  48.5 18.9 %collective-permute-start.1 = (f32[2,2,64,128]{3,2,1,0:T(8,128)S(1)}, f32[2,2,64,128]{3,2,1,0:T(8,128)S(1)}, u32[]{:S(2)}, u32[]{:S(2)}) collective-permute-start(f32[2,2,64,128]{3,2,1,0:T(8,128)S(1)} %get-tuple-element.12), channel_id=1, source_target_pairs={{0,32},{32,64},{64,96},{96,0},{1,33},{33,65},{65,97},{97,1},{2,34}... | collective-permute-start | bytes 393224 | tf_op jit(solution)/shard_map/ppermute | solution.py:254
  60.9 7.7 %collective-permute-start.2 = (f32[2,2,64,128]{3,2,1,0:T(8,128)S(1)}, f32[2,2,64,128]{3,2,1,0:T(8,128)S(1)}, u32[]{:S(2)}, u32[]{:S(2)}) collective-permute-start(f32[2,2,64,128]{3,2,1,0:T(8,128)S(1)} %get-tuple-element.13), channel_id=1, source_target_pairs={{0,128},{128,256},{256,384},{384,0},{1,129},{129,257},{257,385},{3... | collective-permute-start | bytes 393224 | tf_op jit(solution)/shard_map/ppermute | solution.py:255
  64.1 8.3 %collective-permute-start.3 = (f32[2,2,64,128]{3,2,1,0:T(8,128)S(1)}, f32[2,2,64,128]{3,2,1,0:T(8,128)S(1)}, u32[]{:S(2)}, u32[]{:S(2)}) collective-permute-start(f32[2,2,64,128]{3,2,1,0:T(8,128)S(1)} %get-tuple-element.14), channel_id=1, source_target_pairs={{0,160},{32,192},{64,224},{96,128},{128,288},{160,320},{192,352},{... | collective-permute-start | bytes 393224 | tf_op jit(solution)/shard_map/ppermute | solution.py:256

commit v3 on v2

--- a/solution.py
+++ b/solution.py
@@ -11,23 +11,32 @@
 SMEM = pl.BlockSpec(memory_space=pltpu.SMEM)
 
 
-def conv_kernel(half_ref, own_ref, other_ref, weight_ref, keep_ref, y_ref, z_ref, corner_ref, cells, total):
-    step = pl.program_id(0)
-
-    @pl.when(step == 0)
-    def _():
-        half = half_ref[0]
-        for k in range(16):
-            for row in range(4):
-                lanes = pl.ds(row * 128, 128)
-                cells[k, half, :, lanes] = own_ref[k, row]
-                cells[k, 1 - half, :, lanes] = other_ref[k, row]
-        total[...] = jnp.zeros_like(total)
-
-    products = jnp.dot(
-        weight_ref[0], cells[...].reshape(1024, 512), preferred_element_type=F32
-    )
-    lane = lax.broadcasted_iota(jnp.int32, (64, 128), 1)
+def split_kernel(own_ref, first_ref, second_ref):
+    first_ref[...] = own_ref[:8]
+    second_ref[...] = own_ref[8:]
+
+
+def split(own):
+    piece = jax.ShapeDtypeStruct((8, 4, 32, 128), BF16)
+    return pl.pallas_call(
+        split_kernel,
+        in_specs=[VMEM],
+        out_specs=[VMEM] * 2,
+        out_shape=[piece] * 2,
+        compiler_params=pltpu.CompilerParams(vmem_limit_bytes=4 << 20),
+        cost_estimate=pl.CostEstimate(flops=0, bytes_accessed=1 << 20, transcendentals=0),
+        name="split",
+    )(own)
+
+
+ORDER = (0, 2, 1, 3)
+
+
+def place_of(k):
+    return 4 * (k // 4) + ORDER.index(k % 4)
+
+
+def spread_terms(products, lane):
     for dy in range(3):
         for z in range(2):
             for y in range(2):
@@ -36,33 +45,88 @@
                     products[(dy * 3 + dx) * 64 : (dy * 3 + dx + 1) * 64, row * 128 : (row + 1) * 128]
                     for dx in range(3)
                 )
-                term = (
+                yield z + 2, y + 2 - dy, (
                     centre
                     + jnp.where(lane == 0, 0.0, pltpu.roll(before, 1, 1))
                     + jnp.where(lane == 127, 0.0, pltpu.roll(after, 127, 1))
                 )
-                total[z + 2 - step, y + 2 - dy] += term
-
-    @pl.when(step == 2)
+
+
+def own_half_kernel(half_ref, own_ref, weight_ref, total_ref, rest_ref, cells, mine):
+    step = pl.program_id(0)
+
+    @pl.when(step == 0)
     def _():
-        for ref, top, left in ((keep_ref, 0, 0), (y_ref, 0, 2), (z_ref, 2, 0), (corner_ref, 2, 2)):
-            for z in range(2):
-                for y in range(2):
-                    ref[z, y] = total[top + z, left + y]
-
-
-def convolve(half, own, other, weight):
-    whole = lambda shape: pl.BlockSpec(shape, lambda i: (0,) * len(shape))
-    return pl.pallas_call(
-        conv_kernel,
+        for k in range(16):
+            for row in range(4):
+                cells[place_of(k), :, row * 128 : (row + 1) * 128] = own_ref[k, row]
+        total_ref[...] = jnp.zeros_like(total_ref)
+
+    lane = lax.broadcasted_iota(jnp.int32, (64, 128), 1)
+    first = half_ref[0] == 0
+    for r in range(9):
+        rows = slice(r * 64, (r + 1) * 64)
+        for u in range(4):
+            left = weight_ref[0, rows, u * 256 : u * 256 + 128].astype(F32)
+            right = weight_ref[0, rows, u * 256 + 128 : (u + 1) * 256].astype(F32)
+            keep = lane // 32 % 2 == 0
+            even = jnp.where(keep, left, pltpu.roll(right, 32, 1)).astype(BF16)
+            odd = jnp.where(keep, pltpu.roll(left, 96, 1), right).astype(BF16)
+            mine[rows, u * 128 : (u + 1) * 128] = jnp.where(first, even, odd)
+            rest_ref[0, rows, u * 128 : (u + 1) * 128] = jnp.where(first, odd, even)
+
+    products = jnp.dot(mine[...], cells[...].reshape(512, 512), preferred_element_type=F32)
+    for z, y, term in spread_terms(products, lane):
+        total_ref[z - step, y] += term
+
+
+def own_half(half, own, weight):
+    return pl.pallas_call(
+        own_half_kernel,
         grid=(3,),
-        in_specs=[SMEM, VMEM, VMEM, pl.BlockSpec((1, 576, 1024), lambda i: (i, 0, 0))],
-        out_specs=[whole((2, 2, 64, 128))] * 4,
+        in_specs=[SMEM, VMEM, pl.BlockSpec((1, 576, 1024), lambda i: (i, 0, 0))],
+        out_specs=[
+            pl.BlockSpec((4, 4, 64, 128), lambda i: (0, 0, 0, 0)),
+            pl.BlockSpec((1, 576, 512), lambda i: (i, 0, 0)),
+        ],
+        out_shape=[
+            jax.ShapeDtypeStruct((4, 4, 64, 128), F32),
+            jax.ShapeDtypeStruct((3, 576, 512), BF16),
+        ],
+        scratch_shapes=[pltpu.VMEM((16, 32, 512), BF16), pltpu.VMEM((576, 512), BF16)],
+        compiler_params=pltpu.CompilerParams(vmem_limit_bytes=16 << 20),
+        cost_estimate=pl.CostEstimate(flops=1 << 30, bytes_accessed=6 << 20, transcendentals=0),
+        name="own_half",
+    )(half, own, weight)
+
+
+def other_half_kernel(first_ref, second_ref, rest_ref, total_ref, keep_ref, y_ref, z_ref, corner_ref, cells):
+    for k in range(16):
+        for row in range(4):
+            cells[place_of(k), :, row * 128 : (row + 1) * 128] = (first_ref, second_ref)[k // 8][k % 8, row]
+    sums = ((keep_ref, y_ref), (z_ref, corner_ref))
+    for z in range(4):
+        for y in range(4):
+            sums[z // 2][y // 2][z % 2, y % 2] = total_ref[z, y]
+    lane = lax.broadcasted_iota(jnp.int32, (64, 128), 1)
+    for step in range(3):
+        products = jnp.dot(rest_ref[step], cells[...].reshape(512, 512), preferred_element_type=F32)
+        for z, y, term in spread_terms(products, lane):
+            z = z - step
+            sums[z // 2][y // 2][z % 2, y % 2] += term
+
+
+def other_half(first, second, rest, total):
+    return pl.pallas_call(
+        other_half_kernel,
+        in_specs=[VMEM] * 4,
+        out_specs=[VMEM] * 4,
         out_shape=[jax.ShapeDtypeStruct((2, 2, 64, 128), F32)] * 4,
-        scratch_shapes=[pltpu.VMEM((16, 2, 32, 512), BF16), pltpu.VMEM((4, 4, 64, 128), F32)],
+        scratch_shapes=[pltpu.VMEM((16, 32, 512), BF16)],
         compiler_params=pltpu.CompilerParams(vmem_limit_bytes=16 << 20),
-        name="conv",
-    )(half, own, other, weight)
+        cost_estimate=pl.CostEstimate(flops=1 << 30, bytes_accessed=3 << 20, transcendentals=0),
+        name="other_half",
+    )(first, second, rest, total)
 
 
 def gate_kernel(slot_ref, gz_ref, gy_ref, keep_ref, y_ref, z_ref, corner_ref, out_ref, turned, packed):
@@ -145,8 +209,8 @@
 
     def send(dz, dy, slots):
         at = ((gz + dz) % 4) * 4 + (gy + dy) % 4
-        for k, slot in enumerate(slots):
-            sent_ref[at, k] = slot
+        for k in range(len(slots) // 2):
+            sent_ref[at, k] = jnp.concatenate(slots[2 * k : 2 * k + 2], axis=0).astype(BF16)
 
     by_z = [own_ref[k] for k in range(8)]
     by_y = [turned[k] for k in range(8)]
@@ -164,7 +228,7 @@
         out_specs=[VMEM] * 2,
         out_shape=[
             jax.ShapeDtypeStruct((8, 8, 128), F32),
-            jax.ShapeDtypeStruct((16, 6, 8, 128), F32),
+            jax.ShapeDtypeStruct((16, 3, 16, 128), BF16),
         ],
         scratch_shapes=[pltpu.VMEM((16, 512), F32), pltpu.VMEM((8, 8, 128), F32)],
         compiler_params=pltpu.CompilerParams(vmem_limit_bytes=8 << 20),
@@ -197,10 +261,17 @@
     gz, gy = gz_ref[0], gy_ref[0]
     at = lambda dz, dy: ((gz + dz) % 4) * 4 + (gy + dy) % 4
     after, before = at(0, 1), at(0, 3)
-    for k in range(6):
-        across[1, :, k, :] = got_ref[after, k]
-    for k in range(2):
-        across[0, :, 6 + k, :] = got_ref[before, k]
+
+    def slots_from(source, count):
+        for k in range(count // 2):
+            pair = got_ref[source, k].astype(F32)
+            yield pair[:8]
+            yield pair[8:]
+
+    for k, cells in enumerate(slots_from(after, 6)):
+        across[1, :, k, :] = cells
+    for k, cells in enumerate(slots_from(before, 2)):
+        across[0, :, 6 + k, :] = cells
     sub = lax.broadcasted_iota(jnp.int32, (8, 128), 0)
 
     def shortened(cells):
@@ -209,8 +280,8 @@
 
     for side, dy in ((0, 3), (1, 1), (2, 0)):
         change = shortened if side == 1 else lambda cells: cells
-        below = [change(got_ref[at(3, dy), k]) for k in range(2)]
-        above = [change(got_ref[at(1, dy), k]) for k in range(6)]
+        below = [change(cells) for cells in slots_from(at(3, dy), 2)]
+        above = [change(cells) for cells in slots_from(at(1, dy), 6)]
         centre = [own_ref[k] if side == 2 else across[side, k] for k in range(8)]
         for i, fine in enumerate(two_levels(below, centre, above)):
             tall[side, :, i, :] = fine
@@ -240,10 +311,9 @@
     slot = ((lax.axis_index("ring") * 2 + half) % 4).reshape(1)
     gz, gy = (lax.axis_index(axis).reshape(1) for axis in ("gz", "gy"))
     own = lax.all_gather(volume.reshape(4, 32, 128), "ring", axis=0, tiled=False)
-    other = lax.ppermute(own, "half", [(0, 1), (1, 0)])
-    keep, to_y, to_z, to_corner = convolve(
-        half.reshape(1), own, other, conv_weight.reshape(3, 576, 1024)
-    )
+    swapped = [lax.ppermute(piece, "half", [(0, 1), (1, 0)]) for piece in split(own)]
+    total, rest = own_half(half.reshape(1), own, conv_weight.reshape(3, 576, 1024))
+    keep, to_y, to_z, to_corner = other_half(*swapped, rest, total)
     step = [(i, (i + 1) % 4) for i in range(4)]
     both = [(a * 4 + b, c * 4 + d) for a, c in step for b, d in step]
     sent = gate(

time: 111 us -> 107 us (0.964)
  waiting for transfers between devices: 11.8 us -> 7.01 us
  blocking collectives: 69.1 us -> 66.5 us
  starting transfers between devices: 23.5 us -> 25 us
  Pallas kernels: 4.38 us -> 5.79 us
    ppermute x1 -> x2, waiting for transfers between devices: 6.77 us -> 1.36 us  [on_device(): lax.ppermute(piece, 'half', [(0, 1), (1, 0)])]
    ppermute x1 -> x2, starting transfers between devices: 4.64 us -> 6.79 us  [on_device(): lax.ppermute(piece, 'half', [(0, 1), (1, 0)])]
    all_to_all x1, blocking collectives: 25.6 us -> 23.7 us  [on_device(): lax.all_to_all(sent, ('ring', 'half'), split_axis=0, concat_axis=0, tiled...]
    pallas_call x1 -> x3, Pallas kernels: 3 us -> 4.41 us  [the longest x1 3.09 us: own_half(): pl.pallas_call(own_half_kernel, grid=(3,), in_specs=[SMEM, VMEM, pl.Block...]
  transfers between devices with their start and end apart: 4 -> 5, of which waited for: 3 -> 3; matrix products, arithmetic and copies ran while one was open for 0% -> 0% of each run, Pallas kernels for 0% -> 3%
where the time goes in v3:
time: 107 us; the launch traced here: 106 us
  blocking collectives  66.5 us (62%)
  starting transfers between devices  25 us (23%)
  waiting for transfers between devices  7.01 us (7%)
  Pallas kernels  5.79 us (5%)
  local copies, waits for them, and re-layouts  2 us (2%)
    all_gather x1, blocking collectives, on_device(): lax.all_gather(volume.reshape(4, 32, 128), 'ring', axis=0, tiled=False)  32 us
    all_to_all x1, blocking collectives, on_device(): lax.all_to_all(sent, ('ring', 'half'), split_axis=0, concat_axis=0, tiled...  23.7 us
    ppermute x1, starting transfers between devices, on_device(): lax.ppermute(to_y, 'gy', step)  11.8 us
    all_to_all x1, blocking collectives, on_device(): lax.all_to_all(messages, ('gz', 'gy'), split_axis=0, concat_axis=0, tiled...  10.7 us
    ppermute x2, starting transfers between devices, on_device(): lax.ppermute(piece, 'half', [(0, 1), (1, 0)])  6.79 us
    ppermute x1, waiting for transfers between devices, on_device(): lax.ppermute(to_corner, ('gz', 'gy'), both)  3.63 us
    ppermute x1, starting transfers between devices, on_device(): lax.ppermute(to_corner, ('gz', 'gy'), both)  3.22 us
    ppermute x1, starting transfers between devices, on_device(): lax.ppermute(to_z, 'gz', step)  3.2 us
  transfers between devices with their start and end apart: 5, of which 3 were waited for; matrix products, arithmetic and copies ran while one was open for 0% of the time, Pallas kernels for 3%

profile of v3, /device:TPU:1, one launch (start us, length us, event | category | flops | bytes accessed | tf_op | source)
XLA Modules:
  0.0 106.4 jit_solution(3119041396210810157)
XLA Ops:
  0.0 32.0 %all_gather.3.own_ref = bf16[16,4,32,128]{3,2,1,0:T(8,128)(2,1)S(1)} all-gather(bf16[1,4,32,128]{3,2,1,0:T(8,128)(2,1)} %bitcast.7), channel_id=1, replica_groups=mesh['gz'=4,'gy'=4,'ring'=16,'half'=2] {'ring'}, dimensions={0}, use_global_device_ids=true | all-gather | bytes 557056 | tf_op jit(solution)/shard_map/all_gather | solution.py:313
  32.1 4.7 %collective-permute-start = (bf16[8,4,32,128]{3,2,1,0:T(8,128)(2,1)S(1)}, bf16[8,4,32,128]{3,2,1,0:T(8,128)(2,1)S(1)}, u32[]{:S(2)}, u32[]{:S(2)}) collective-permute-start(bf16[8,4,32,128]{3,2,1,0:T(8,128)(2,1)S(1)} %get-tuple-element.15), channel_id=1, source_target_pairs={{0,1},{1,0},{2,3},{3,2},{4,5},{5,4},{6,7},{7,6},{8,9},{9,8},{10,11... | collective-permute-start | bytes 786440 | tf_op jit(solution)/shard_map/ppermute | solution.py:314
  36.7 2.1 %collective-permute-start.1 = (bf16[8,4,32,128]{3,2,1,0:T(8,128)(2,1)S(1)}, bf16[8,4,32,128]{3,2,1,0:T(8,128)(2,1)S(1)}, u32[]{:S(2)}, u32[]{:S(2)}) collective-permute-start(bf16[8,4,32,128]{3,2,1,0:T(8,128)(2,1)S(1)} %get-tuple-element.16), channel_id=1, source_target_pairs={{0,1},{1,0},{2,3},{3,2},{4,5},{5,4},{6,7},{7,6},{8,9},{9,8},{10,11... | collective-permute-start | bytes 786440 | tf_op jit(solution)/shard_map/ppermute | solution.py:314
  38.9 0.0 copy-start
  38.9 2.0 %copy-done = bf16[27,2,32,1024]{3,2,1,0:T(8,128)(2,1)S(1)} copy-done((bf16[27,2,32,1024]{3,2,1,0:T(8,128)(2,1)S(1)}, bf16[27,2,32,1024]{3,2,1,0:T(8,128)(2,1)}, u32[]{:S(2)}) %copy-start) | copy-done | bytes 3538968
  40.9 0.0 copy-start.1
  40.9 3.1 %own_half.1 = (f32[4,4,64,128]{3,2,1,0:T(8,128)S(1)}, bf16[3,576,512]{2,1,0:T(8,128)(2,1)S(1)}) custom-call(s32[1]{0:T(128)} %bitcast.4.half_ref, bf16[16,4,32,128]{3,2,1,0:T(8,128)(2,1)S(1)} %all_gather.3.own_ref, bf16[3,576,1024]{2,1,0:T(8,128)(2,1)S(1)} %bitcast.6), custom_call_target="tpu_custom_call" | custom-call | flops 1073741824 | bytes 6291456 | tf_op jit(solution)/shard_map/own_half/pallas_call | solution.py:84
  44.0 0.0 collective-permute-done.first_ref
  44.0 1.4 %collective-permute-done.1.second_ref = bf16[8,4,32,128]{3,2,1,0:T(8,128)(2,1)S(1)} collective-permute-done((bf16[8,4,32,128]{3,2,1,0:T(8,128)(2,1)S(1)}, bf16[8,4,32,128]{3,2,1,0:T(8,128)(2,1)S(1)}, u32[]{:S(2)}, u32[]{:S(2)}) %collective-permute-start.1) | collective-permute-done | bytes 262176 | tf_op jit(solution)/shard_map/ppermute | solution.py:314
  45.4 1.3 %other_half.1 = (f32[2,2,64,128]{3,2,1,0:T(8,128)S(1)}, f32[2,2,64,128]{3,2,1,0:T(8,128)S(1)}, f32[2,2,64,128]{3,2,1,0:T(8,128)S(1)}, f32[2,2,64,128]{3,2,1,0:T(8,128)S(1)}) custom-call(bf16[8,4,32,128]{3,2,1,0:T(8,128)(2,1)S(1)} %collective-permute-done.first_ref, bf16[8,4,32,128]{3,2,1,0:T(8,128)(2,1)S(1)} %collective-permute-done.1.second_ref, ...), custom_call_target="tpu_custom_call" | custom-call | flops 1073741824 | bytes 3145728 | tf_op jit(solution)/shard_map/other_half/pallas_call | solution.py:120
  46.7 11.8 %collective-permute-start.2 = (f32[2,2,64,128]{3,2,1,0:T(8,128)S(1)}, f32[2,2,64,128]{3,2,1,0:T(8,128)S(1)}, u32[]{:S(2)}, u32[]{:S(2)}) collective-permute-start(f32[2,2,64,128]{3,2,1,0:T(8,128)S(1)} %get-tuple-element.20), channel_id=1, source_target_pairs={{0,32},{32,64},{64,96},{96,0},{1,33},{33,65},{65,97},{97,1},{2,34}... | collective-permute-start | bytes 393224 | tf_op jit(solution)/shard_map/ppermute | solution.py:324
  58.4 3.2 %collective-permute-start.3 = (f32[2,2,64,128]{3,2,1,0:T(8,128)S(1)}, f32[2,2,64,128]{3,2,1,0:T(8,128)S(1)}, u32[]{:S(2)}, u32[]{:S(2)}) collective-permute-start(f32[2,2,64,128]{3,2,1,0:T(8,128)S(1)} %get-tuple-element.21), channel_id=1, source_target_pairs={{0,128},{128,256},{256,384},{384,0},{1,129},{129,257},{257,385},{3... | collective-permute-start | bytes 393224 | tf_op jit(solution)/shard_map/ppermute | solution.py:325
  61.7 3.2 %collective-permute-start.4 = (f32[2,2,64,128]{3,2,1,0:T(8,128)S(1)}, f32[2,2,64,128]{3,2,1,0:T(8,128)S(1)}, u32[]{:S(2)}, u32[]{:S(2)}) collective-permute-start(f32[2,2,64,128]{3,2,1,0:T(8,128)S(1)} %get-tuple-element.22), channel_id=1, source_target_pairs={{0,160},{32,192},{64,224},{96,128},{128,288},{160,320},{192,352},{... | collective-permute-start | bytes 393224 | tf_op jit(solution)/shard_map/ppermute | solution.py:326
  64.9 0.0 collective-permute-done.2.y_ref
  64.9 2.0 %collective-permute-done.3.z_ref = f32[2,2,64,128]{3,2,1,0:T(8,128)S(1)} collective-permute-done((f32[2,2,64,128]{3,2,1,0:T(8,128)S(1)}, f32[2,2,64,128]{3,2,1,0:T(8,128)S(1)}, u32[]{:S(2)}, u32[]{:S(2)}) %collective-permute-start.3) | collective-permute-done | bytes 131104 | tf_op jit(solution)/shard_map/ppermute | solution.py:325
  66.9 3.6 %collective-permute-done.4.corner_ref = f32[2,2,64,128]{3,2,1,0:T(8,128)S(1)} collective-permute-done((f32[2,2,64,128]{3,2,1,0:T(8,128)S(1)}, f32[2,2,64,128]{3,2,1,0:T(8,128)S(1)}, u32[]{:S(2)}, u32[]{:S(2)}) %collective-permute-start.4) | collective-permute-done | bytes 131104 | tf_op jit(solution)/shard_map/ppermute | solution.py:326
  70.6 0.2 gate.1
  70.8 23.7 %all_to_all.10.parts_ref = bf16[32,16,128]{2,1,0:T(8,128)(2,1)S(1)} all-to-all(bf16[32,16,128]{2,1,0:T(8,128)(2,1)S(1)} %gate.1), channel_id=1, replica_groups=mesh['gz'=4,'gy'=4,'ring'=16,'half'=2] {'ring','half'}, dimensions={0} | all-to-all | bytes 262144 | tf_op jit(solution)/shard_map/all_to_all | solution.py:328
  94.5 0.0 copy-done.1
  94.5 0.4 project.1
  94.9 10.7 %all_to_all.11.got_ref = bf16[16,3,16,128]{3,2,1,0:T(8,128)(2,1)S(1)} all-to-all(bf16[16,3,16,128]{3,2,1,0:T(8,128)(2,1)S(1)} %get-tuple-element.24), channel_id=1, replica_groups=mesh['gz'=4,'gy'=4,'ring'=16,'half'=2] {'gz','gy'}, dimensions={0} | all-to-all | bytes 393216 | tf_op jit(solution)/shard_map/all_to_all | solution.py:330
  105.6 0.7 lift.1
  (1 shorter events, 0.0 us)
Async XLA Ops:
  32.1 11.9 %collective-permute-start = (bf16[8,4,32,128]{3,2,1,0:T(8,128)(2,1)S(1)}, bf16[8,4,32,128]{3,2,1,0:T(8,128)(2,1)S(1)}, u32[]{:S(2)}, u32[]{:S(2)}) collective-permute-start(bf16[8,4,32,128]{3,2,1,0:T(8,128)(2,1)S(1)} %get-tuple-element.15), channel_id=1, source_target_pairs={{0,1},{1,0},{2,3},{3,2},{4,5},{5,4},{6,7},{7,6},{8,9},{9,8},{10,11... | collective-permute-start | bytes 786440 | tf_op jit(solution)/shard_map/ppermute | solution.py:314
  36.7 8.6 %collective-permute-start.1 = (bf16[8,4,32,128]{3,2,1,0:T(8,128)(2,1)S(1)}, bf16[8,4,32,128]{3,2,1,0:T(8,128)(2,1)S(1)}, u32[]{:S(2)}, u32[]{:S(2)}) collective-permute-start(bf16[8,4,32,128]{3,2,1,0:T(8,128)(2,1)S(1)} %get-tuple-element.16), channel_id=1, source_target_pairs={{0,1},{1,0},{2,3},{3,2},{4,5},{5,4},{6,7},{7,6},{8,9},{9,8},{10,11... | collective-permute-start | bytes 786440 | tf_op jit(solution)/shard_map/ppermute | solution.py:314
  38.9 2.0 %copy-start = (bf16[27,2,32,1024]{3,2,1,0:T(8,128)(2,1)S(1)}, bf16[27,2,32,1024]{3,2,1,0:T(8,128)(2,1)}, u32[]{:S(2)}) copy-start(bf16[27,2,32,1024]{3,2,1,0:T(8,128)(2,1)} %param.4) | copy-start | bytes 10616836
  40.9 53.6 %copy-start.1 = (bf16[1024,512]{1,0:T(8,128)(2,1)S(1)}, bf16[1024,512]{1,0:T(8,128)(2,1)}, u32[]{:S(2)}) copy-start(bf16[1024,512]{1,0:T(8,128)(2,1)} %proj_ref.1) | copy-start | bytes 3145732
  46.7 18.2 %collective-permute-start.2 = (f32[2,2,64,128]{3,2,1,0:T(8,128)S(1)}, f32[2,2,64,128]{3,2,1,0:T(8,128)S(1)}, u32[]{:S(2)}, u32[]{:S(2)}) collective-permute-start(f32[2,2,64,128]{3,2,1,0:T(8,128)S(1)} %get-tuple-element.20), channel_id=1, source_target_pairs={{0,32},{32,64},{64,96},{96,0},{1,33},{33,65},{65,97},{97,1},{2,34}... | collective-permute-start | bytes 393224 | tf_op jit(solution)/shard_map/ppermute | solution.py:324
  58.4 8.5 %collective-permute-start.3 = (f32[2,2,64,128]{3,2,1,0:T(8,128)S(1)}, f32[2,2,64,128]{3,2,1,0:T(8,128)S(1)}, u32[]{:S(2)}, u32[]{:S(2)}) collective-permute-start(f32[2,2,64,128]{3,2,1,0:T(8,128)S(1)} %get-tuple-element.21), channel_id=1, source_target_pairs={{0,128},{128,256},{256,384},{384,0},{1,129},{129,257},{257,385},{3... | collective-permute-start | bytes 393224 | tf_op jit(solution)/shard_map/ppermute | solution.py:325
  61.7 8.9 %collective-permute-start.4 = (f32[2,2,64,128]{3,2,1,0:T(8,128)S(1)}, f32[2,2,64,128]{3,2,1,0:T(8,128)S(1)}, u32[]{:S(2)}, u32[]{:S(2)}) collective-permute-start(f32[2,2,64,128]{3,2,1,0:T(8,128)S(1)} %get-tuple-element.22), channel_id=1, source_target_pairs={{0,160},{32,192},{64,224},{96,128},{128,288},{160,320},{192,352},{... | collective-permute-start | bytes 393224 | tf_op jit(solution)/shard_map/ppermute | solution.py:326

commit v4 on v3

--- a/solution.py
+++ b/solution.py
@@ -9,24 +9,6 @@
 BF16 = jnp.bfloat16
 VMEM = pl.BlockSpec(memory_space=pltpu.VMEM)
 SMEM = pl.BlockSpec(memory_space=pltpu.SMEM)
-
-
-def split_kernel(own_ref, first_ref, second_ref):
-    first_ref[...] = own_ref[:8]
-    second_ref[...] = own_ref[8:]
-
-
-def split(own):
-    piece = jax.ShapeDtypeStruct((8, 4, 32, 128), BF16)
-    return pl.pallas_call(
-        split_kernel,
-        in_specs=[VMEM],
-        out_specs=[VMEM] * 2,
-        out_shape=[piece] * 2,
-        compiler_params=pltpu.CompilerParams(vmem_limit_bytes=4 << 20),
-        cost_estimate=pl.CostEstimate(flops=0, bytes_accessed=1 << 20, transcendentals=0),
-        name="split",
-    )(own)
 
 
 ORDER = (0, 2, 1, 3)
@@ -100,10 +82,10 @@
     )(half, own, weight)
 
 
-def other_half_kernel(first_ref, second_ref, rest_ref, total_ref, keep_ref, y_ref, z_ref, corner_ref, cells):
+def other_half_kernel(other_ref, rest_ref, total_ref, keep_ref, y_ref, z_ref, corner_ref, cells):
     for k in range(16):
         for row in range(4):
-            cells[place_of(k), :, row * 128 : (row + 1) * 128] = (first_ref, second_ref)[k // 8][k % 8, row]
+            cells[place_of(k), :, row * 128 : (row + 1) * 128] = other_ref[k, row]
     sums = ((keep_ref, y_ref), (z_ref, corner_ref))
     for z in range(4):
         for y in range(4):
@@ -116,17 +98,17 @@
             sums[z // 2][y // 2][z % 2, y % 2] += term
 
 
-def other_half(first, second, rest, total):
+def other_half(other, rest, total):
     return pl.pallas_call(
         other_half_kernel,
-        in_specs=[VMEM] * 4,
+        in_specs=[VMEM] * 3,
         out_specs=[VMEM] * 4,
         out_shape=[jax.ShapeDtypeStruct((2, 2, 64, 128), F32)] * 4,
         scratch_shapes=[pltpu.VMEM((16, 32, 512), BF16)],
         compiler_params=pltpu.CompilerParams(vmem_limit_bytes=16 << 20),
         cost_estimate=pl.CostEstimate(flops=1 << 30, bytes_accessed=3 << 20, transcendentals=0),
         name="other_half",
-    )(first, second, rest, total)
+    )(other, rest, total)
 
 
 def gate_kernel(slot_ref, gz_ref, gy_ref, keep_ref, y_ref, z_ref, corner_ref, out_ref, turned, packed):
@@ -310,10 +292,11 @@
     half = lax.axis_index("half")
     slot = ((lax.axis_index("ring") * 2 + half) % 4).reshape(1)
     gz, gy = (lax.axis_index(axis).reshape(1) for axis in ("gz", "gy"))
-    own = lax.all_gather(volume.reshape(4, 32, 128), "ring", axis=0, tiled=False)
-    swapped = [lax.ppermute(piece, "half", [(0, 1), (1, 0)]) for piece in split(own)]
+    copies = jnp.broadcast_to(volume.reshape(1, 4, 32, 128), (16, 4, 32, 128))
+    own = lax.all_to_all(copies, "ring", split_axis=0, concat_axis=0, tiled=True)
+    other = lax.ppermute(own, "half", [(0, 1), (1, 0)])
     total, rest = own_half(half.reshape(1), own, conv_weight.reshape(3, 576, 1024))
-    keep, to_y, to_z, to_corner = other_half(*swapped, rest, total)
+    keep, to_y, to_z, to_corner = other_half(other, rest, total)
     step = [(i, (i + 1) % 4) for i in range(4)]
     both = [(a * 4 + b, c * 4 + d) for a, c in step for b, d in step]
     sent = gate(

time: 107 us -> 116 us (1.084)
  blocking collectives: 66.5 us -> 78.4 us
  starting transfers between devices: 25 us -> 22.2 us
    all_to_all x0 -> x1, blocking collectives: none -> 38.5 us  [on_device(): lax.all_to_all(copies, 'ring', split_axis=0, concat_axis=0, tiled=True)]
    all_gather x1 -> x0, blocking collectives: 32 us -> none  [on_device(): lax.all_gather(volume.reshape(4, 32, 128), 'ring', axis=0, tiled=False)]
    all_to_all x1, blocking collectives: 23.7 us -> 29.9 us  [on_device(): lax.all_to_all(sent, ('ring', 'half'), split_axis=0, concat_axis=0, tiled...]
    ppermute x2 -> x1, starting transfers between devices: 6.79 us -> 4.64 us  [on_device(): other = lax.ppermute(own, 'half', [(0, 1), (1, 0)])]
  transfers between devices with their start and end apart: 5 -> 4, of which waited for: 3 -> 3; matrix products, arithmetic and copies ran while one was open for 0% -> 0% of each run, Pallas kernels for 3% -> 3%
where the time goes in v4:
time: 116 us
  blocking collectives  78.4 us (68%)
  starting transfers between devices  22.2 us (19%)
  waiting for transfers between devices  6.73 us (6%)
  Pallas kernels  5.76 us (5%)
  local copies, waits for them, and re-layouts  2.85 us (2%)
    all_to_all x1, blocking collectives, on_device(): lax.all_to_all(copies, 'ring', split_axis=0, concat_axis=0, tiled=True)  38.5 us
    all_to_all x1, blocking collectives, on_device(): lax.all_to_all(sent, ('ring', 'half'), split_axis=0, concat_axis=0, tiled...  29.9 us
    ppermute x1, starting transfers between devices, on_device(): lax.ppermute(to_y, 'gy', step)  11.2 us
    all_to_all x1, blocking collectives, on_device(): lax.all_to_all(messages, ('gz', 'gy'), split_axis=0, concat_axis=0, tiled...  9.89 us
    ppermute x1, starting transfers between devices, on_device(): other = lax.ppermute(own, 'half', [(0, 1), (1, 0)])  4.64 us
    ppermute x1, waiting for transfers between devices, on_device(): lax.ppermute(to_corner, ('gz', 'gy'), both)  3.82 us
    ppermute x1, starting transfers between devices, on_device(): lax.ppermute(to_corner, ('gz', 'gy'), both)  3.21 us
    ppermute x1, starting transfers between devices, on_device(): lax.ppermute(to_z, 'gz', step)  3.2 us
  transfers between devices with their start and end apart: 4, of which 3 were waited for; matrix products, arithmetic and copies ran while one was open for 0% of the time, Pallas kernels for 3%

profile of v4, /device:TPU:1, one launch (start us, length us, event | category | flops | bytes accessed | tf_op | source)
XLA Modules:
  0.0 116.0 jit_solution(9677072389488142645)
XLA Ops:
  0.0 0.8 broadcast_in_dim.8
  0.9 38.5 %all_to_all.15.own_ref = bf16[16,4,32,128]{3,2,1,0:T(8,128)(2,1)S(1)} all-to-all(bf16[16,4,32,128]{3,2,1,0:T(8,128)(2,1)S(1)} %broadcast_in_dim.8), channel_id=1, replica_groups=mesh['gz'=4,'gy'=4,'ring'=16,'half'=2] {'ring'}, dimensions={0} | all-to-all | bytes 1048576 | tf_op jit(solution)/shard_map/all_to_all | solution.py:296
  39.4 4.6 %collective-permute-start = (bf16[16,4,32,128]{3,2,1,0:T(8,128)(2,1)S(1)}, bf16[16,4,32,128]{3,2,1,0:T(8,128)(2,1)S(1)}, u32[]{:S(2)}, u32[]{:S(2)}) collective-permute-start(bf16[16,4,32,128]{3,2,1,0:T(8,128)(2,1)S(1)} %all_to_all.15.own_ref), channel_id=1, source_target_pairs={{0,1},{1,0},{2,3},{3,2},{4,5},{5,4},{6,7},{7,6},{8,9},{9,8},{10,11... | collective-permute-start | bytes 1572872 | tf_op jit(solution)/shard_map/ppermute | solution.py:297
  44.1 0.0 copy-start
  44.1 2.0 %copy-done = bf16[27,2,32,1024]{3,2,1,0:T(8,128)(2,1)S(1)} copy-done((bf16[27,2,32,1024]{3,2,1,0:T(8,128)(2,1)S(1)}, bf16[27,2,32,1024]{3,2,1,0:T(8,128)(2,1)}, u32[]{:S(2)}) %copy-start) | copy-done | bytes 3538968
  46.1 0.0 copy-start.1
  46.1 3.1 %own_half.1 = (f32[4,4,64,128]{3,2,1,0:T(8,128)S(1)}, bf16[3,576,512]{2,1,0:T(8,128)(2,1)S(1)}) custom-call(s32[1]{0:T(128)} %bitcast.4.half_ref, bf16[16,4,32,128]{3,2,1,0:T(8,128)(2,1)S(1)} %all_to_all.15.own_ref, bf16[3,576,1024]{2,1,0:T(8,128)(2,1)S(1)} %bitcast.6), custom_call_target="tpu_custom_call" | custom-call | flops 1073741824 | bytes 6291456 | tf_op jit(solution)/shard_map/own_half/pallas_call | solution.py:66
  49.2 1.7 %collective-permute-done.other_ref = bf16[16,4,32,128]{3,2,1,0:T(8,128)(2,1)S(1)} collective-permute-done((bf16[16,4,32,128]{3,2,1,0:T(8,128)(2,1)S(1)}, bf16[16,4,32,128]{3,2,1,0:T(8,128)(2,1)S(1)}, u32[]{:S(2)}, u32[]{:S(2)}) %collective-permute-start) | collective-permute-done | bytes 524320 | tf_op jit(solution)/shard_map/ppermute | solution.py:297
  50.8 1.3 %other_half.1 = (f32[2,2,64,128]{3,2,1,0:T(8,128)S(1)}, f32[2,2,64,128]{3,2,1,0:T(8,128)S(1)}, f32[2,2,64,128]{3,2,1,0:T(8,128)S(1)}, f32[2,2,64,128]{3,2,1,0:T(8,128)S(1)}) custom-call(bf16[16,4,32,128]{3,2,1,0:T(8,128)(2,1)S(1)} %collective-permute-done.other_ref, bf16[3,576,512]{2,1,0:T(8,128)(2,1)S(1)} %get-tuple-element.13.rest_ref, ...), custom_call_target="tpu_custom_call" | custom-call | flops 1073741824 | bytes 3145728 | tf_op jit(solution)/shard_map/other_half/pallas_call | solution.py:102
  52.1 11.2 %collective-permute-start.1 = (f32[2,2,64,128]{3,2,1,0:T(8,128)S(1)}, f32[2,2,64,128]{3,2,1,0:T(8,128)S(1)}, u32[]{:S(2)}, u32[]{:S(2)}) collective-permute-start(f32[2,2,64,128]{3,2,1,0:T(8,128)S(1)} %get-tuple-element.16), channel_id=1, source_target_pairs={{0,32},{32,64},{64,96},{96,0},{1,33},{33,65},{65,97},{97,1},{2,34}... | collective-permute-start | bytes 393224 | tf_op jit(solution)/shard_map/ppermute | solution.py:307
  63.3 3.2 %collective-permute-start.2 = (f32[2,2,64,128]{3,2,1,0:T(8,128)S(1)}, f32[2,2,64,128]{3,2,1,0:T(8,128)S(1)}, u32[]{:S(2)}, u32[]{:S(2)}) collective-permute-start(f32[2,2,64,128]{3,2,1,0:T(8,128)S(1)} %get-tuple-element.17), channel_id=1, source_target_pairs={{0,128},{128,256},{256,384},{384,0},{1,129},{129,257},{257,385},{3... | collective-permute-start | bytes 393224 | tf_op jit(solution)/shard_map/ppermute | solution.py:308
  66.5 3.2 %collective-permute-start.3 = (f32[2,2,64,128]{3,2,1,0:T(8,128)S(1)}, f32[2,2,64,128]{3,2,1,0:T(8,128)S(1)}, u32[]{:S(2)}, u32[]{:S(2)}) collective-permute-start(f32[2,2,64,128]{3,2,1,0:T(8,128)S(1)} %get-tuple-element.18), channel_id=1, source_target_pairs={{0,160},{32,192},{64,224},{96,128},{128,288},{160,320},{192,352},{... | collective-permute-start | bytes 393224 | tf_op jit(solution)/shard_map/ppermute | solution.py:309
  69.7 0.0 collective-permute-done.1.y_ref
  69.8 1.2 %collective-permute-done.2.z_ref = f32[2,2,64,128]{3,2,1,0:T(8,128)S(1)} collective-permute-done((f32[2,2,64,128]{3,2,1,0:T(8,128)S(1)}, f32[2,2,64,128]{3,2,1,0:T(8,128)S(1)}, u32[]{:S(2)}, u32[]{:S(2)}) %collective-permute-start.2) | collective-permute-done | bytes 131104 | tf_op jit(solution)/shard_map/ppermute | solution.py:308
  71.0 3.8 %collective-permute-done.3.corner_ref = f32[2,2,64,128]{3,2,1,0:T(8,128)S(1)} collective-permute-done((f32[2,2,64,128]{3,2,1,0:T(8,128)S(1)}, f32[2,2,64,128]{3,2,1,0:T(8,128)S(1)}, u32[]{:S(2)}, u32[]{:S(2)}) %collective-permute-start.3) | collective-permute-done | bytes 131104 | tf_op jit(solution)/shard_map/ppermute | solution.py:309
  74.8 0.2 gate.1
  75.1 29.9 %all_to_all.16.parts_ref = bf16[32,16,128]{2,1,0:T(8,128)(2,1)S(1)} all-to-all(bf16[32,16,128]{2,1,0:T(8,128)(2,1)S(1)} %gate.1), channel_id=1, replica_groups=mesh['gz'=4,'gy'=4,'ring'=16,'half'=2] {'ring','half'}, dimensions={0} | all-to-all | bytes 262144 | tf_op jit(solution)/shard_map/all_to_all | solution.py:311
  105.0 0.0 copy-done.1
  105.0 0.4 project.1
  105.4 9.9 %all_to_all.17.got_ref = bf16[16,3,16,128]{3,2,1,0:T(8,128)(2,1)S(1)} all-to-all(bf16[16,3,16,128]{3,2,1,0:T(8,128)(2,1)S(1)} %get-tuple-element.20), channel_id=1, replica_groups=mesh['gz'=4,'gy'=4,'ring'=16,'half'=2] {'gz','gy'}, dimensions={0} | all-to-all | bytes 393216 | tf_op jit(solution)/shard_map/all_to_all | solution.py:313
  115.3 0.7 lift.1
Async XLA Ops:
  39.4 11.4 %collective-permute-start = (bf16[16,4,32,128]{3,2,1,0:T(8,128)(2,1)S(1)}, bf16[16,4,32,128]{3,2,1,0:T(8,128)(2,1)S(1)}, u32[]{:S(2)}, u32[]{:S(2)}) collective-permute-start(bf16[16,4,32,128]{3,2,1,0:T(8,128)(2,1)S(1)} %all_to_all.15.own_ref), channel_id=1, source_target_pairs={{0,1},{1,0},{2,3},{3,2},{4,5},{5,4},{6,7},{7,6},{8,9},{9,8},{10,11... | collective-permute-start | bytes 1572872 | tf_op jit(solution)/shard_map/ppermute | solution.py:297
  44.1 2.0 %copy-start = (bf16[27,2,32,1024]{3,2,1,0:T(8,128)(2,1)S(1)}, bf16[27,2,32,1024]{3,2,1,0:T(8,128)(2,1)}, u32[]{:S(2)}) copy-start(bf16[27,2,32,1024]{3,2,1,0:T(8,128)(2,1)} %param.4) | copy-start | bytes 10616836
  46.1 58.9 %copy-start.1 = (bf16[1024,512]{1,0:T(8,128)(2,1)S(1)}, bf16[1024,512]{1,0:T(8,128)(2,1)}, u32[]{:S(2)}) copy-start(bf16[1024,512]{1,0:T(8,128)(2,1)} %proj_ref.1) | copy-start | bytes 3145732
  52.1 17.6 %collective-permute-start.1 = (f32[2,2,64,128]{3,2,1,0:T(8,128)S(1)}, f32[2,2,64,128]{3,2,1,0:T(8,128)S(1)}, u32[]{:S(2)}, u32[]{:S(2)}) collective-permute-start(f32[2,2,64,128]{3,2,1,0:T(8,128)S(1)} %get-tuple-element.16), channel_id=1, source_target_pairs={{0,32},{32,64},{64,96},{96,0},{1,33},{33,65},{65,97},{97,1},{2,34}... | collective-permute-start | bytes 393224 | tf_op jit(solution)/shard_map/ppermute | solution.py:307
  63.3 7.7 %collective-permute-start.2 = (f32[2,2,64,128]{3,2,1,0:T(8,128)S(1)}, f32[2,2,64,128]{3,2,1,0:T(8,128)S(1)}, u32[]{:S(2)}, u32[]{:S(2)}) collective-permute-start(f32[2,2,64,128]{3,2,1,0:T(8,128)S(1)} %get-tuple-element.17), channel_id=1, source_target_pairs={{0,128},{128,256},{256,384},{384,0},{1,129},{129,257},{257,385},{3... | collective-permute-start | bytes 393224 | tf_op jit(solution)/shard_map/ppermute | solution.py:308
  66.5 8.3 %collective-permute-start.3 = (f32[2,2,64,128]{3,2,1,0:T(8,128)S(1)}, f32[2,2,64,128]{3,2,1,0:T(8,128)S(1)}, u32[]{:S(2)}, u32[]{:S(2)}) collective-permute-start(f32[2,2,64,128]{3,2,1,0:T(8,128)S(1)} %get-tuple-element.18), channel_id=1, source_target_pairs={{0,160},{32,192},{64,224},{96,128},{128,288},{160,320},{192,352},{... | collective-permute-start | bytes 393224 | tf_op jit(solution)/shard_map/ppermute | solution.py:309

commit v5 on v4

--- a/solution.py
+++ b/solution.py
@@ -4,6 +4,7 @@
 from jax.experimental import pallas as pl
 from jax.experimental.pallas import tpu as pltpu
 from jax.sharding import Mesh, PartitionSpec as P
+
 
 F32 = jnp.float32
 BF16 = jnp.bfloat16
@@ -292,22 +293,16 @@
     half = lax.axis_index("half")
     slot = ((lax.axis_index("ring") * 2 + half) % 4).reshape(1)
     gz, gy = (lax.axis_index(axis).reshape(1) for axis in ("gz", "gy"))
-    copies = jnp.broadcast_to(volume.reshape(1, 4, 32, 128), (16, 4, 32, 128))
-    own = lax.all_to_all(copies, "ring", split_axis=0, concat_axis=0, tiled=True)
+    own = lax.all_gather(volume.reshape(4, 32, 128), "ring", axis=0, tiled=False)
     other = lax.ppermute(own, "half", [(0, 1), (1, 0)])
     total, rest = own_half(half.reshape(1), own, conv_weight.reshape(3, 576, 1024))
     keep, to_y, to_z, to_corner = other_half(other, rest, total)
     step = [(i, (i + 1) % 4) for i in range(4)]
     both = [(a * 4 + b, c * 4 + d) for a, c in step for b, d in step]
-    sent = gate(
-        slot,
-        gz,
-        gy,
-        keep,
-        lax.ppermute(to_y, "gy", step),
-        lax.ppermute(to_z, "gz", step),
-        lax.ppermute(to_corner, ("gz", "gy"), both),
-    )
+    from_corner = lax.ppermute(to_corner, ("gz", "gy"), both)
+    from_z = lax.ppermute(to_z, "gz", step)
+    from_y = lax.ppermute(to_y, "gy", step)
+    sent = gate(slot, gz, gy, keep, from_y, from_z, from_corner)
     parts = lax.all_to_all(sent, ("ring", "half"), split_axis=0, concat_axis=0, tiled=True)
     coefficients, messages = project(gz, gy, parts, proj_weight)
     got = lax.all_to_all(messages, ("gz", "gy"), split_axis=0, concat_axis=0, tiled=True)

time: 116 us -> 106 us (0.914)
  blocking collectives: 78.4 us -> 67.5 us
  starting transfers between devices: 22.2 us -> 23.5 us
    all_to_all x1 -> x0, blocking collectives: 38.5 us -> none  [on_device(): lax.all_to_all(copies, 'ring', split_axis=0, concat_axis=0, tiled=True)]
    all_gather x0 -> x1, blocking collectives: none -> 32 us  [on_device(): lax.all_gather(volume.reshape(4, 32, 128), 'ring', axis=0, tiled=False)]
    all_to_all x1, blocking collectives: 29.9 us -> 25.6 us  [on_device(): lax.all_to_all(sent, ('ring', 'half'), split_axis=0, concat_axis=0, tiled...]
    ppermute x3, starting transfers between devices: 17.6 us -> 18.8 us  [the longest x1 12.4 us: on_device(): from_y = lax.ppermute(to_y, 'gy', step)]
where the time goes in v5:
time: 106 us
  blocking collectives  67.5 us (64%)
  starting transfers between devices  23.5 us (22%)
  waiting for transfers between devices  6.72 us (6%)
  Pallas kernels  5.76 us (5%)
  local copies, waits for them, and re-layouts  2 us (2%)
    all_gather x1, blocking collectives, on_device(): lax.all_gather(volume.reshape(4, 32, 128), 'ring', axis=0, tiled=False)  32 us
    all_to_all x1, blocking collectives, on_device(): lax.all_to_all(sent, ('ring', 'half'), split_axis=0, concat_axis=0, tiled...  25.6 us
    ppermute x1, starting transfers between devices, on_device(): from_y = lax.ppermute(to_y, 'gy', step)  12.4 us
    all_to_all x1, blocking collectives, on_device(): lax.all_to_all(messages, ('gz', 'gy'), split_axis=0, concat_axis=0, tiled...  9.89 us
    ppermute x1, starting transfers between devices, on_device(): other = lax.ppermute(own, 'half', [(0, 1), (1, 0)])  4.64 us
    ppermute x1, waiting for transfers between devices, on_device(): from_corner = lax.ppermute(to_corner, ('gz', 'gy'), both)  3.82 us
    ppermute x1, starting transfers between devices, on_device(): from_corner = lax.ppermute(to_corner, ('gz', 'gy'), both)  3.21 us
    ppermute x1, starting transfers between devices, on_device(): from_z = lax.ppermute(to_z, 'gz', step)  3.2 us
  transfers between devices with their start and end apart: 4, of which 3 were waited for; matrix products, arithmetic and copies ran while one was open for 0% of the time, Pallas kernels for 3%

profile of v5, /device:TPU:1, one launch (start us, length us, event | category | flops | bytes accessed | tf_op | source)
XLA Modules:
  0.0 105.5 jit_solution(9102282249044470379)
XLA Ops:
  0.0 32.0 %all_gather.3.own_ref = bf16[16,4,32,128]{3,2,1,0:T(8,128)(2,1)S(1)} all-gather(bf16[1,4,32,128]{3,2,1,0:T(8,128)(2,1)} %bitcast.7), channel_id=1, replica_groups=mesh['gz'=4,'gy'=4,'ring'=16,'half'=2] {'ring'}, dimensions={0}, use_global_device_ids=true | all-gather | bytes 557056 | tf_op jit(solution)/shard_map/all_gather | solution.py:296
  32.0 4.6 %collective-permute-start = (bf16[16,4,32,128]{3,2,1,0:T(8,128)(2,1)S(1)}, bf16[16,4,32,128]{3,2,1,0:T(8,128)(2,1)S(1)}, u32[]{:S(2)}, u32[]{:S(2)}) collective-permute-start(bf16[16,4,32,128]{3,2,1,0:T(8,128)(2,1)S(1)} %all_gather.3.own_ref), channel_id=1, source_target_pairs={{0,1},{1,0},{2,3},{3,2},{4,5},{5,4},{6,7},{7,6},{8,9},{9,8},{10,11... | collective-permute-start | bytes 1572872 | tf_op jit(solution)/shard_map/ppermute | solution.py:297
  36.7 0.0 copy-start
  36.7 2.0 %copy-done = bf16[27,2,32,1024]{3,2,1,0:T(8,128)(2,1)S(1)} copy-done((bf16[27,2,32,1024]{3,2,1,0:T(8,128)(2,1)S(1)}, bf16[27,2,32,1024]{3,2,1,0:T(8,128)(2,1)}, u32[]{:S(2)}) %copy-start) | copy-done | bytes 3538968
  38.7 0.0 copy-start.1
  38.7 3.1 %own_half.1 = (f32[4,4,64,128]{3,2,1,0:T(8,128)S(1)}, bf16[3,576,512]{2,1,0:T(8,128)(2,1)S(1)}) custom-call(s32[1]{0:T(128)} %bitcast.4.half_ref, bf16[16,4,32,128]{3,2,1,0:T(8,128)(2,1)S(1)} %all_gather.3.own_ref, bf16[3,576,1024]{2,1,0:T(8,128)(2,1)S(1)} %bitcast.6), custom_call_target="tpu_custom_call" | custom-call | flops 1073741824 | bytes 6291456 | tf_op jit(solution)/shard_map/own_half/pallas_call | solution.py:67
  41.8 1.7 %collective-permute-done.other_ref = bf16[16,4,32,128]{3,2,1,0:T(8,128)(2,1)S(1)} collective-permute-done((bf16[16,4,32,128]{3,2,1,0:T(8,128)(2,1)S(1)}, bf16[16,4,32,128]{3,2,1,0:T(8,128)(2,1)S(1)}, u32[]{:S(2)}, u32[]{:S(2)}) %collective-permute-start) | collective-permute-done | bytes 524320 | tf_op jit(solution)/shard_map/ppermute | solution.py:297
  43.5 1.3 %other_half.1 = (f32[2,2,64,128]{3,2,1,0:T(8,128)S(1)}, f32[2,2,64,128]{3,2,1,0:T(8,128)S(1)}, f32[2,2,64,128]{3,2,1,0:T(8,128)S(1)}, f32[2,2,64,128]{3,2,1,0:T(8,128)S(1)}) custom-call(bf16[16,4,32,128]{3,2,1,0:T(8,128)(2,1)S(1)} %collective-permute-done.other_ref, bf16[3,576,512]{2,1,0:T(8,128)(2,1)S(1)} %get-tuple-element.13.rest_ref, ...), custom_call_target="tpu_custom_call" | custom-call | flops 1073741824 | bytes 3145728 | tf_op jit(solution)/shard_map/other_half/pallas_call | solution.py:103
  44.8 12.4 %collective-permute-start.1 = (f32[2,2,64,128]{3,2,1,0:T(8,128)S(1)}, f32[2,2,64,128]{3,2,1,0:T(8,128)S(1)}, u32[]{:S(2)}, u32[]{:S(2)}) collective-permute-start(f32[2,2,64,128]{3,2,1,0:T(8,128)S(1)} %get-tuple-element.16), channel_id=1, source_target_pairs={{0,32},{32,64},{64,96},{96,0},{1,33},{33,65},{65,97},{97,1},{2,34}... | collective-permute-start | bytes 393224 | tf_op jit(solution)/shard_map/ppermute | solution.py:304
  57.2 3.2 %collective-permute-start.2 = (f32[2,2,64,128]{3,2,1,0:T(8,128)S(1)}, f32[2,2,64,128]{3,2,1,0:T(8,128)S(1)}, u32[]{:S(2)}, u32[]{:S(2)}) collective-permute-start(f32[2,2,64,128]{3,2,1,0:T(8,128)S(1)} %get-tuple-element.17), channel_id=1, source_target_pairs={{0,128},{128,256},{256,384},{384,0},{1,129},{129,257},{257,385},{3... | collective-permute-start | bytes 393224 | tf_op jit(solution)/shard_map/ppermute | solution.py:303
  60.4 3.2 %collective-permute-start.3 = (f32[2,2,64,128]{3,2,1,0:T(8,128)S(1)}, f32[2,2,64,128]{3,2,1,0:T(8,128)S(1)}, u32[]{:S(2)}, u32[]{:S(2)}) collective-permute-start(f32[2,2,64,128]{3,2,1,0:T(8,128)S(1)} %get-tuple-element.18), channel_id=1, source_target_pairs={{0,160},{32,192},{64,224},{96,128},{128,288},{160,320},{192,352},{... | collective-permute-start | bytes 393224 | tf_op jit(solution)/shard_map/ppermute | solution.py:302
  63.6 0.0 collective-permute-done.1.y_ref
  63.6 1.2 %collective-permute-done.2.z_ref = f32[2,2,64,128]{3,2,1,0:T(8,128)S(1)} collective-permute-done((f32[2,2,64,128]{3,2,1,0:T(8,128)S(1)}, f32[2,2,64,128]{3,2,1,0:T(8,128)S(1)}, u32[]{:S(2)}, u32[]{:S(2)}) %collective-permute-start.2) | collective-permute-done | bytes 131104 | tf_op jit(solution)/shard_map/ppermute | solution.py:303
  64.9 3.8 %collective-permute-done.3.corner_ref = f32[2,2,64,128]{3,2,1,0:T(8,128)S(1)} collective-permute-done((f32[2,2,64,128]{3,2,1,0:T(8,128)S(1)}, f32[2,2,64,128]{3,2,1,0:T(8,128)S(1)}, u32[]{:S(2)}, u32[]{:S(2)}) %collective-permute-start.3) | collective-permute-done | bytes 131104 | tf_op jit(solution)/shard_map/ppermute | solution.py:302
  68.7 0.2 gate.1
  68.9 25.6 %all_to_all.10.parts_ref = bf16[32,16,128]{2,1,0:T(8,128)(2,1)S(1)} all-to-all(bf16[32,16,128]{2,1,0:T(8,128)(2,1)S(1)} %gate.1), channel_id=1, replica_groups=mesh['gz'=4,'gy'=4,'ring'=16,'half'=2] {'ring','half'}, dimensions={0} | all-to-all | bytes 262144 | tf_op jit(solution)/shard_map/all_to_all | solution.py:306
  94.5 0.0 copy-done.1
  94.5 0.4 project.1
  94.9 9.9 %all_to_all.11.got_ref = bf16[16,3,16,128]{3,2,1,0:T(8,128)(2,1)S(1)} all-to-all(bf16[16,3,16,128]{3,2,1,0:T(8,128)(2,1)S(1)} %get-tuple-element.20), channel_id=1, replica_groups=mesh['gz'=4,'gy'=4,'ring'=16,'half'=2] {'gz','gy'}, dimensions={0} | all-to-all | bytes 393216 | tf_op jit(solution)/shard_map/all_to_all | solution.py:308
  104.8 0.7 lift.1
Async XLA Ops:
  32.0 11.4 %collective-permute-start = (bf16[16,4,32,128]{3,2,1,0:T(8,128)(2,1)S(1)}, bf16[16,4,32,128]{3,2,1,0:T(8,128)(2,1)S(1)}, u32[]{:S(2)}, u32[]{:S(2)}) collective-permute-start(bf16[16,4,32,128]{3,2,1,0:T(8,128)(2,1)S(1)} %all_gather.3.own_ref), channel_id=1, source_target_pairs={{0,1},{1,0},{2,3},{3,2},{4,5},{5,4},{6,7},{7,6},{8,9},{9,8},{10,11... | collective-permute-start | bytes 1572872 | tf_op jit(solution)/shard_map/ppermute | solution.py:297
  36.7 2.0 %copy-start = (bf16[27,2,32,1024]{3,2,1,0:T(8,128)(2,1)S(1)}, bf16[27,2,32,1024]{3,2,1,0:T(8,128)(2,1)}, u32[]{:S(2)}) copy-start(bf16[27,2,32,1024]{3,2,1,0:T(8,128)(2,1)} %param.4) | copy-start | bytes 10616836
  38.7 55.8 %copy-start.1 = (bf16[1024,512]{1,0:T(8,128)(2,1)S(1)}, bf16[1024,512]{1,0:T(8,128)(2,1)}, u32[]{:S(2)}) copy-start(bf16[1024,512]{1,0:T(8,128)(2,1)} %proj_ref.1) | copy-start | bytes 3145732
  44.8 18.9 %collective-permute-start.1 = (f32[2,2,64,128]{3,2,1,0:T(8,128)S(1)}, f32[2,2,64,128]{3,2,1,0:T(8,128)S(1)}, u32[]{:S(2)}, u32[]{:S(2)}) collective-permute-start(f32[2,2,64,128]{3,2,1,0:T(8,128)S(1)} %get-tuple-element.16), channel_id=1, source_target_pairs={{0,32},{32,64},{64,96},{96,0},{1,33},{33,65},{65,97},{97,1},{2,34}... | collective-permute-start | bytes 393224 | tf_op jit(solution)/shard_map/ppermute | solution.py:304
  57.2 7.7 %collective-permute-start.2 = (f32[2,2,64,128]{3,2,1,0:T(8,128)S(1)}, f32[2,2,64,128]{3,2,1,0:T(8,128)S(1)}, u32[]{:S(2)}, u32[]{:S(2)}) collective-permute-start(f32[2,2,64,128]{3,2,1,0:T(8,128)S(1)} %get-tuple-element.17), channel_id=1, source_target_pairs={{0,128},{128,256},{256,384},{384,0},{1,129},{129,257},{257,385},{3... | collective-permute-start | bytes 393224 | tf_op jit(solution)/shard_map/ppermute | solution.py:303
  60.4 8.3 %collective-permute-start.3 = (f32[2,2,64,128]{3,2,1,0:T(8,128)S(1)}, f32[2,2,64,128]{3,2,1,0:T(8,128)S(1)}, u32[]{:S(2)}, u32[]{:S(2)}) collective-permute-start(f32[2,2,64,128]{3,2,1,0:T(8,128)S(1)} %get-tuple-element.18), channel_id=1, source_target_pairs={{0,160},{32,192},{64,224},{96,128},{128,288},{160,320},{192,352},{... | collective-permute-start | bytes 393224 | tf_op jit(solution)/shard_map/ppermute | solution.py:302

commit v6 on v5

--- a/solution.py
+++ b/solution.py
@@ -112,10 +112,9 @@
     )(other, rest, total)
 
 
-def gate_kernel(slot_ref, gz_ref, gy_ref, keep_ref, y_ref, z_ref, corner_ref, out_ref, turned, packed):
-    slot = slot_ref[0]
+def gate_kernel(gz_ref, gy_ref, keep_ref, y_ref, z_ref, corner_ref, out_ref, turned):
     inside = [jnp.where(ref[0] > 0, 1.0, 0.0) for ref in (gz_ref, gy_ref)]
-    group = lax.broadcasted_iota(jnp.int32, (128, 128), 0) // 32
+    pieces = []
     for z in range(2):
         for y in range(2):
             z_own, z_before = ((inside[0], 1.0), (1.0, inside[0]))[z]
@@ -127,24 +126,22 @@
                 + corner_ref[z, y] * (z_before * y_before)
             )
             gate, value = conv_out[:32], conv_out[32:]
-            gated = gate / (1.0 + jnp.exp(-gate)) * value
-            spread = jnp.where(group == slot, jnp.concatenate([gated] * 4, axis=0), 0.0)
-            turned[...] = spread.T
-            for i in range(4):
-                packed[pl.ds(i * 4 + z * 2 + y, 32, stride=16), :] = turned[pl.ds(i, 32, stride=4), :]
-    out_ref[...] = packed[...].reshape(32, 16, 128).astype(BF16)
-
-
-def gate(slot, gz, gy, *pieces):
+            pieces.append(gate / (1.0 + jnp.exp(-gate)) * value)
+    turned[...] = jnp.concatenate(pieces, axis=0).T
+    for k in range(32):
+        out_ref[k] = turned[4 * k : 4 * k + 4, :].astype(BF16)
+
+
+def gate(gz, gy, *pieces):
     return pl.pallas_call(
         gate_kernel,
-        in_specs=[SMEM] * 3 + [VMEM] * 4,
+        in_specs=[SMEM] * 2 + [VMEM] * 4,
         out_specs=VMEM,
-        out_shape=jax.ShapeDtypeStruct((32, 16, 128), BF16),
-        scratch_shapes=[pltpu.VMEM((128, 128), F32), pltpu.VMEM((512, 128), F32)],
+        out_shape=jax.ShapeDtypeStruct((32, 4, 128), BF16),
+        scratch_shapes=[pltpu.VMEM((128, 128), F32)],
         compiler_params=pltpu.CompilerParams(vmem_limit_bytes=4 << 20),
         name="gate",
-    )(slot, gz, gy, *pieces)
+    )(gz, gy, *pieces)
 
 
 S, D = (0, 1), (2, 3)
@@ -159,27 +156,30 @@
     return [slots[4 + D[h]] for h in range(2)]
 
 
-def project_kernel(gz_ref, gy_ref, parts_ref, proj_ref, own_ref, sent_ref, held, turned):
-    chunks = []
+def swapped_blocks(rows, block, place):
+    merged = None
+    for i in range(4):
+        shift = ((i - place) % 4) * 32
+        moved = rows[i] if shift == 0 else pltpu.roll(rows[i], shift, 1)
+        merged = moved if merged is None else jnp.where(block == i, moved, merged)
+    return merged
+
+
+def project_kernel(gz_ref, gy_ref, parts_ref, proj_ref, own_ref, sent_ref, gathered, held, turned):
+    block = lax.broadcasted_iota(jnp.int32, (4, 128), 1) // 32
     for k in range(8):
-        chunk = parts_ref[4 * k].astype(F32)
-        for i in range(1, 4):
-            chunk = chunk + parts_ref[4 * k + i].astype(F32)
-        chunks.append(chunk.astype(BF16))
-    held[...] = jnp.dot(
-        jnp.concatenate(chunks, axis=1), proj_ref[...], preferred_element_type=F32
-    )
-    block = lax.broadcasted_iota(jnp.int32, (4, 128), 1) // 32
+        rows = [parts_ref[4 * k + i].astype(F32) for i in range(4)]
+        for cell in range(4):
+            gathered[cell * 4 : cell * 4 + 4, k * 128 : (k + 1) * 128] = swapped_blocks(rows, block, cell)
+    product = jnp.dot(gathered[...].astype(BF16), proj_ref[...], preferred_element_type=F32)
     for b1 in range(4):
-        rows = [held[i * 4 : (i + 1) * 4, b1 * 128 : (b1 + 1) * 128] for i in range(4)]
+        held[b1] = product[:, b1 * 128 : (b1 + 1) * 128]
+    for b1 in range(4):
+        rows = [held[b1, pl.ds(i, 4, stride=4), :] for i in range(4)]
         hz1, hy1 = b1 // 2, b1 % 2
         for b2 in range(4):
             hz2, hy2 = b2 // 2, b2 % 2
-            merged = None
-            for i in range(4):
-                shift = ((i - b2) % 4) * 32
-                moved = rows[i] if shift == 0 else pltpu.roll(rows[i], shift, 1)
-                merged = moved if merged is None else jnp.where(block == i, moved, merged)
+            merged = swapped_blocks(rows, block, b2)
             for z in range(2):
                 for y in range(2):
                     row = merged[z * 2 + y : z * 2 + y + 1, :]
@@ -213,7 +213,11 @@
             jax.ShapeDtypeStruct((8, 8, 128), F32),
             jax.ShapeDtypeStruct((16, 3, 16, 128), BF16),
         ],
-        scratch_shapes=[pltpu.VMEM((16, 512), F32), pltpu.VMEM((8, 8, 128), F32)],
+        scratch_shapes=[
+            pltpu.VMEM((16, 1024), F32),
+            pltpu.VMEM((4, 16, 128), F32),
+            pltpu.VMEM((8, 8, 128), F32),
+        ],
         compiler_params=pltpu.CompilerParams(vmem_limit_bytes=8 << 20),
         name="project",
     )(gz, gy, parts, proj_weight)
@@ -291,7 +295,6 @@
 
 def on_device(volume, conv_weight, proj_weight):
     half = lax.axis_index("half")
-    slot = ((lax.axis_index("ring") * 2 + half) % 4).reshape(1)
     gz, gy = (lax.axis_index(axis).reshape(1) for axis in ("gz", "gy"))
     own = lax.all_gather(volume.reshape(4, 32, 128), "ring", axis=0, tiled=False)
     other = lax.ppermute(own, "half", [(0, 1), (1, 0)])
@@ -302,7 +305,7 @@
     from_corner = lax.ppermute(to_corner, ("gz", "gy"), both)
     from_z = lax.ppermute(to_z, "gz", step)
     from_y = lax.ppermute(to_y, "gy", step)
-    sent = gate(slot, gz, gy, keep, from_y, from_z, from_corner)
+    sent = gate(gz, gy, keep, from_y, from_z, from_corner)
     parts = lax.all_to_all(sent, ("ring", "half"), split_axis=0, concat_axis=0, tiled=True)
     coefficients, messages = project(gz, gy, parts, proj_weight)
     got = lax.all_to_all(messages, ("gz", "gy"), split_axis=0, concat_axis=0, tiled=True)

time: 106 us -> 103 us (0.972)
  blocking collectives: 67.5 us -> 65.2 us
    all_to_all x1, blocking collectives: 25.6 us -> 22.7 us  [on_device(): lax.all_to_all(sent, ('ring', 'half'), split_axis=0, concat_axis=0, tiled...]
where the time goes in v6:
time: 103 us
  blocking collectives  65.2 us (63%)
  starting transfers between devices  23.5 us (23%)
  waiting for transfers between devices  6.73 us (7%)
  Pallas kernels  5.72 us (6%)
  local copies, waits for them, and re-layouts  2 us (2%)
    all_gather x1, blocking collectives, on_device(): lax.all_gather(volume.reshape(4, 32, 128), 'ring', axis=0, tiled=False)  32 us
    all_to_all x1, blocking collectives, on_device(): lax.all_to_all(sent, ('ring', 'half'), split_axis=0, concat_axis=0, tiled...  22.7 us
    ppermute x1, starting transfers between devices, on_device(): from_y = lax.ppermute(to_y, 'gy', step)  12.4 us
    all_to_all x1, blocking collectives, on_device(): lax.all_to_all(messages, ('gz', 'gy'), split_axis=0, concat_axis=0, tiled...  10.4 us
    ppermute x1, starting transfers between devices, on_device(): other = lax.ppermute(own, 'half', [(0, 1), (1, 0)])  4.64 us
    ppermute x1, waiting for transfers between devices, on_device(): from_corner = lax.ppermute(to_corner, ('gz', 'gy'), both)  3.82 us
    ppermute x1, starting transfers between devices, on_device(): from_corner = lax.ppermute(to_corner, ('gz', 'gy'), both)  3.21 us
    ppermute x1, starting transfers between devices, on_device(): from_z = lax.ppermute(to_z, 'gz', step)  3.2 us
  transfers between devices with their start and end apart: 4, of which 3 were waited for; matrix products, arithmetic and copies ran while one was open for 0% of the time, Pallas kernels for 3%

profile of v6, /device:TPU:1, one launch (start us, length us, event | category | flops | bytes accessed | tf_op | source)
XLA Modules:
  0.0 103.2 jit_solution(11986563791322818678)
XLA Ops:
  0.0 32.0 %all_gather.3.own_ref = bf16[16,4,32,128]{3,2,1,0:T(8,128)(2,1)S(1)} all-gather(bf16[1,4,32,128]{3,2,1,0:T(8,128)(2,1)} %bitcast.6), channel_id=1, replica_groups=mesh['gz'=4,'gy'=4,'ring'=16,'half'=2] {'ring'}, dimensions={0}, use_global_device_ids=true | all-gather | bytes 557056 | tf_op jit(solution)/shard_map/all_gather | solution.py:299
  32.0 4.6 %collective-permute-start = (bf16[16,4,32,128]{3,2,1,0:T(8,128)(2,1)S(1)}, bf16[16,4,32,128]{3,2,1,0:T(8,128)(2,1)S(1)}, u32[]{:S(2)}, u32[]{:S(2)}) collective-permute-start(bf16[16,4,32,128]{3,2,1,0:T(8,128)(2,1)S(1)} %all_gather.3.own_ref), channel_id=1, source_target_pairs={{0,1},{1,0},{2,3},{3,2},{4,5},{5,4},{6,7},{7,6},{8,9},{9,8},{10,11... | collective-permute-start | bytes 1572872 | tf_op jit(solution)/shard_map/ppermute | solution.py:300
  36.7 0.0 copy-start
  36.7 2.0 %copy-done = bf16[27,2,32,1024]{3,2,1,0:T(8,128)(2,1)S(1)} copy-done((bf16[27,2,32,1024]{3,2,1,0:T(8,128)(2,1)S(1)}, bf16[27,2,32,1024]{3,2,1,0:T(8,128)(2,1)}, u32[]{:S(2)}) %copy-start) | copy-done | bytes 3538968
  38.7 0.0 copy-start.1
  38.7 3.1 %own_half.1 = (f32[4,4,64,128]{3,2,1,0:T(8,128)S(1)}, bf16[3,576,512]{2,1,0:T(8,128)(2,1)S(1)}) custom-call(s32[1]{0:T(128)} %bitcast.3.half_ref, bf16[16,4,32,128]{3,2,1,0:T(8,128)(2,1)S(1)} %all_gather.3.own_ref, bf16[3,576,1024]{2,1,0:T(8,128)(2,1)S(1)} %bitcast.5), custom_call_target="tpu_custom_call" | custom-call | flops 1073741824 | bytes 6291456 | tf_op jit(solution)/shard_map/own_half/pallas_call | solution.py:67
  41.8 1.7 %collective-permute-done.other_ref = bf16[16,4,32,128]{3,2,1,0:T(8,128)(2,1)S(1)} collective-permute-done((bf16[16,4,32,128]{3,2,1,0:T(8,128)(2,1)S(1)}, bf16[16,4,32,128]{3,2,1,0:T(8,128)(2,1)S(1)}, u32[]{:S(2)}, u32[]{:S(2)}) %collective-permute-start) | collective-permute-done | bytes 524320 | tf_op jit(solution)/shard_map/ppermute | solution.py:300
  43.5 1.3 %other_half.1 = (f32[2,2,64,128]{3,2,1,0:T(8,128)S(1)}, f32[2,2,64,128]{3,2,1,0:T(8,128)S(1)}, f32[2,2,64,128]{3,2,1,0:T(8,128)S(1)}, f32[2,2,64,128]{3,2,1,0:T(8,128)S(1)}) custom-call(bf16[16,4,32,128]{3,2,1,0:T(8,128)(2,1)S(1)} %collective-permute-done.other_ref, bf16[3,576,512]{2,1,0:T(8,128)(2,1)S(1)} %get-tuple-element.13.rest_ref, ...), custom_call_target="tpu_custom_call" | custom-call | flops 1073741824 | bytes 3145728 | tf_op jit(solution)/shard_map/other_half/pallas_call | solution.py:103
  44.8 12.4 %collective-permute-start.1 = (f32[2,2,64,128]{3,2,1,0:T(8,128)S(1)}, f32[2,2,64,128]{3,2,1,0:T(8,128)S(1)}, u32[]{:S(2)}, u32[]{:S(2)}) collective-permute-start(f32[2,2,64,128]{3,2,1,0:T(8,128)S(1)} %get-tuple-element.16), channel_id=1, source_target_pairs={{0,32},{32,64},{64,96},{96,0},{1,33},{33,65},{65,97},{97,1},{2,34}... | collective-permute-start | bytes 393224 | tf_op jit(solution)/shard_map/ppermute | solution.py:307
  57.2 3.2 %collective-permute-start.2 = (f32[2,2,64,128]{3,2,1,0:T(8,128)S(1)}, f32[2,2,64,128]{3,2,1,0:T(8,128)S(1)}, u32[]{:S(2)}, u32[]{:S(2)}) collective-permute-start(f32[2,2,64,128]{3,2,1,0:T(8,128)S(1)} %get-tuple-element.17), channel_id=1, source_target_pairs={{0,128},{128,256},{256,384},{384,0},{1,129},{129,257},{257,385},{3... | collective-permute-start | bytes 393224 | tf_op jit(solution)/shard_map/ppermute | solution.py:306
  60.4 3.2 %collective-permute-start.3 = (f32[2,2,64,128]{3,2,1,0:T(8,128)S(1)}, f32[2,2,64,128]{3,2,1,0:T(8,128)S(1)}, u32[]{:S(2)}, u32[]{:S(2)}) collective-permute-start(f32[2,2,64,128]{3,2,1,0:T(8,128)S(1)} %get-tuple-element.18), channel_id=1, source_target_pairs={{0,160},{32,192},{64,224},{96,128},{128,288},{160,320},{192,352},{... | collective-permute-start | bytes 393224 | tf_op jit(solution)/shard_map/ppermute | solution.py:305
  63.6 0.0 collective-permute-done.1.y_ref
  63.6 1.3 %collective-permute-done.2.z_ref = f32[2,2,64,128]{3,2,1,0:T(8,128)S(1)} collective-permute-done((f32[2,2,64,128]{3,2,1,0:T(8,128)S(1)}, f32[2,2,64,128]{3,2,1,0:T(8,128)S(1)}, u32[]{:S(2)}, u32[]{:S(2)}) %collective-permute-start.2) | collective-permute-done | bytes 131104 | tf_op jit(solution)/shard_map/ppermute | solution.py:306
  64.9 3.8 %collective-permute-done.3.corner_ref = f32[2,2,64,128]{3,2,1,0:T(8,128)S(1)} collective-permute-done((f32[2,2,64,128]{3,2,1,0:T(8,128)S(1)}, f32[2,2,64,128]{3,2,1,0:T(8,128)S(1)}, u32[]{:S(2)}, u32[]{:S(2)}) %collective-permute-start.3) | collective-permute-done | bytes 131104 | tf_op jit(solution)/shard_map/ppermute | solution.py:305
  68.7 0.1 gate.1
  68.8 22.7 %all_to_all.10.parts_ref = bf16[32,4,128]{2,1,0:T(4,128)(2,1)S(1)} all-to-all(bf16[32,4,128]{2,1,0:T(4,128)(2,1)S(1)} %gate.1), channel_id=1, replica_groups=mesh['gz'=4,'gy'=4,'ring'=16,'half'=2] {'ring','half'}, dimensions={0} | all-to-all | bytes 65536 | tf_op jit(solution)/shard_map/all_to_all | solution.py:309
  91.6 0.0 copy-done.1
  91.6 0.4 project.1
  92.0 10.4 %all_to_all.11.got_ref = bf16[16,3,16,128]{3,2,1,0:T(8,128)(2,1)S(1)} all-to-all(bf16[16,3,16,128]{3,2,1,0:T(8,128)(2,1)S(1)} %get-tuple-element.20), channel_id=1, replica_groups=mesh['gz'=4,'gy'=4,'ring'=16,'half'=2] {'gz','gy'}, dimensions={0} | all-to-all | bytes 393216 | tf_op jit(solution)/shard_map/all_to_all | solution.py:311
  102.4 0.7 lift.1
Async XLA Ops:
  32.0 11.4 %collective-permute-start = (bf16[16,4,32,128]{3,2,1,0:T(8,128)(2,1)S(1)}, bf16[16,4,32,128]{3,2,1,0:T(8,128)(2,1)S(1)}, u32[]{:S(2)}, u32[]{:S(2)}) collective-permute-start(bf16[16,4,32,128]{3,2,1,0:T(8,128)(2,1)S(1)} %all_gather.3.own_ref), channel_id=1, source_target_pairs={{0,1},{1,0},{2,3},{3,2},{4,5},{5,4},{6,7},{7,6},{8,9},{9,8},{10,11... | collective-permute-start | bytes 1572872 | tf_op jit(solution)/shard_map/ppermute | solution.py:300
  36.7 2.0 %copy-start = (bf16[27,2,32,1024]{3,2,1,0:T(8,128)(2,1)S(1)}, bf16[27,2,32,1024]{3,2,1,0:T(8,128)(2,1)}, u32[]{:S(2)}) copy-start(bf16[27,2,32,1024]{3,2,1,0:T(8,128)(2,1)} %param.4) | copy-start | bytes 10616836
  38.7 52.9 %copy-start.1 = (bf16[1024,512]{1,0:T(8,128)(2,1)S(1)}, bf16[1024,512]{1,0:T(8,128)(2,1)}, u32[]{:S(2)}) copy-start(bf16[1024,512]{1,0:T(8,128)(2,1)} %proj_ref.1) | copy-start | bytes 3145732
  44.8 18.9 %collective-permute-start.1 = (f32[2,2,64,128]{3,2,1,0:T(8,128)S(1)}, f32[2,2,64,128]{3,2,1,0:T(8,128)S(1)}, u32[]{:S(2)}, u32[]{:S(2)}) collective-permute-start(f32[2,2,64,128]{3,2,1,0:T(8,128)S(1)} %get-tuple-element.16), channel_id=1, source_target_pairs={{0,32},{32,64},{64,96},{96,0},{1,33},{33,65},{65,97},{97,1},{2,34}... | collective-permute-start | bytes 393224 | tf_op jit(solution)/shard_map/ppermute | solution.py:307
  57.2 7.7 %collective-permute-start.2 = (f32[2,2,64,128]{3,2,1,0:T(8,128)S(1)}, f32[2,2,64,128]{3,2,1,0:T(8,128)S(1)}, u32[]{:S(2)}, u32[]{:S(2)}) collective-permute-start(f32[2,2,64,128]{3,2,1,0:T(8,128)S(1)} %get-tuple-element.17), channel_id=1, source_target_pairs={{0,128},{128,256},{256,384},{384,0},{1,129},{129,257},{257,385},{3... | collective-permute-start | bytes 393224 | tf_op jit(solution)/shard_map/ppermute | solution.py:306
  60.4 8.3 %collective-permute-start.3 = (f32[2,2,64,128]{3,2,1,0:T(8,128)S(1)}, f32[2,2,64,128]{3,2,1,0:T(8,128)S(1)}, u32[]{:S(2)}, u32[]{:S(2)}) collective-permute-start(f32[2,2,64,128]{3,2,1,0:T(8,128)S(1)} %get-tuple-element.18), channel_id=1, source_target_pairs={{0,160},{32,192},{64,224},{96,128},{128,288},{160,320},{192,352},{... | collective-permute-start | bytes 393224 | tf_op jit(solution)/shard_map/ppermute | solution.py:305

commit v7 on v6

--- a/solution.py
+++ b/solution.py
@@ -83,20 +83,32 @@
     )(half, own, weight)
 
 
-def other_half_kernel(other_ref, rest_ref, total_ref, keep_ref, y_ref, z_ref, corner_ref, cells):
+def other_half_kernel(other_ref, rest_ref, total_ref, keep_ref, y_ref, z_ref, corner_ref, cells, sides):
     for k in range(16):
         for row in range(4):
             cells[place_of(k), :, row * 128 : (row + 1) * 128] = other_ref[k, row]
     sums = ((keep_ref, y_ref), (z_ref, corner_ref))
+    for part in range(3):
+        sides[part] = jnp.zeros_like(sides[part])
+    for step in range(3):
+        products = jnp.dot(rest_ref[step], cells[...].reshape(512, 512), preferred_element_type=F32)
+        for dy in range(3):
+            for z in range(2):
+                for y in range(2):
+                    row = z * 2 + y
+                    for dx in range(3):
+                        sides[dx, z + 2 - step, y + 2 - dy] += products[
+                            (dy * 3 + dx) * 64 : (dy * 3 + dx + 1) * 64, row * 128 : (row + 1) * 128
+                        ]
+    lane = lax.broadcasted_iota(jnp.int32, (64, 128), 1)
     for z in range(4):
         for y in range(4):
-            sums[z // 2][y // 2][z % 2, y % 2] = total_ref[z, y]
-    lane = lax.broadcasted_iota(jnp.int32, (64, 128), 1)
-    for step in range(3):
-        products = jnp.dot(rest_ref[step], cells[...].reshape(512, 512), preferred_element_type=F32)
-        for z, y, term in spread_terms(products, lane):
-            z = z - step
-            sums[z // 2][y // 2][z % 2, y % 2] += term
+            sums[z // 2][y // 2][z % 2, y % 2] = (
+                total_ref[z, y]
+                + sides[1, z, y]
+                + jnp.where(lane == 0, 0.0, pltpu.roll(sides[0, z, y], 1, 1))
+                + jnp.where(lane == 127, 0.0, pltpu.roll(sides[2, z, y], 127, 1))
+            )
 
 
 def other_half(other, rest, total):
@@ -105,7 +117,7 @@
         in_specs=[VMEM] * 3,
         out_specs=[VMEM] * 4,
         out_shape=[jax.ShapeDtypeStruct((2, 2, 64, 128), F32)] * 4,
-        scratch_shapes=[pltpu.VMEM((16, 32, 512), BF16)],
+        scratch_shapes=[pltpu.VMEM((16, 32, 512), BF16), pltpu.VMEM((3, 4, 4, 64, 128), F32)],
         compiler_params=pltpu.CompilerParams(vmem_limit_bytes=16 << 20),
         cost_estimate=pl.CostEstimate(flops=1 << 30, bytes_accessed=3 << 20, transcendentals=0),
         name="other_half",
@@ -296,7 +308,7 @@
 def on_device(volume, conv_weight, proj_weight):
     half = lax.axis_index("half")
     gz, gy = (lax.axis_index(axis).reshape(1) for axis in ("gz", "gy"))
-    own = lax.all_gather(volume.reshape(4, 32, 128), "ring", axis=0, tiled=False)
+    own = lax.all_gather(volume.reshape(128, 128), "ring", axis=0, tiled=True).reshape(16, 4, 32, 128)
     other = lax.ppermute(own, "half", [(0, 1), (1, 0)])
     total, rest = own_half(half.reshape(1), own, conv_weight.reshape(3, 576, 1024))
     keep, to_y, to_z, to_corner = other_half(other, rest, total)

time: 103 us -> 103 us (level)
  no operation moved by 1% of the time
where the time goes in v7:
time: 103 us
  blocking collectives  65.2 us (63%)
  starting transfers between devices  23.5 us (23%)
  waiting for transfers between devices  6.73 us (7%)
  Pallas kernels  5.68 us (6%)
  local copies, waits for them, and re-layouts  2 us (2%)
    all_gather x1, blocking collectives, on_device(): lax.all_gather(volume.reshape(128, 128), 'ring', axis=0, tiled=True)  32 us
    all_to_all x1, blocking collectives, on_device(): lax.all_to_all(sent, ('ring', 'half'), split_axis=0, concat_axis=0, tiled...  22.7 us
    ppermute x1, starting transfers between devices, on_device(): from_y = lax.ppermute(to_y, 'gy', step)  12.4 us
    all_to_all x1, blocking collectives, on_device(): lax.all_to_all(messages, ('gz', 'gy'), split_axis=0, concat_axis=0, tiled...  10.4 us
    ppermute x1, starting transfers between devices, on_device(): other = lax.ppermute(own, 'half', [(0, 1), (1, 0)])  4.64 us
    ppermute x1, waiting for transfers between devices, on_device(): from_corner = lax.ppermute(to_corner, ('gz', 'gy'), both)  3.82 us
    ppermute x1, starting transfers between devices, on_device(): from_corner = lax.ppermute(to_corner, ('gz', 'gy'), both)  3.21 us
    ppermute x1, starting transfers between devices, on_device(): from_z = lax.ppermute(to_z, 'gz', step)  3.2 us
  transfers between devices with their start and end apart: 4, of which 3 were waited for; matrix products, arithmetic and copies ran while one was open for 0% of the time, Pallas kernels for 3%

profile of v7, /device:TPU:1, one launch (start us, length us, event | category | flops | bytes accessed | tf_op | source)
XLA Modules:
  0.0 103.1 jit_solution(15778995258742718098)
XLA Ops:
  0.0 32.0 %all_gather.3 = bf16[2048,128]{1,0:T(8,128)(2,1)S(1)} all-gather(bf16[128,128]{1,0:T(8,128)(2,1)} %bitcast.9), channel_id=1, replica_groups=mesh['gz'=4,'gy'=4,'ring'=16,'half'=2] {'ring'}, dimensions={0}, use_global_device_ids=true | all-gather | bytes 557056 | tf_op jit(solution)/shard_map/all_gather | solution.py:311
  32.0 4.6 %collective-permute-start = (bf16[16,4,32,128]{3,2,1,0:T(8,128)(2,1)S(1)}, bf16[16,4,32,128]{3,2,1,0:T(8,128)(2,1)S(1)}, u32[]{:S(2)}, u32[]{:S(2)}) collective-permute-start(bf16[16,4,32,128]{3,2,1,0:T(8,128)(2,1)S(1)} %bitcast.7), channel_id=1, source_target_pairs={{0,1},{1,0},{2,3},{3,2},{4,5},{5,4},{6,7},{7,6},{8,9},{9,8},{10,11... | collective-permute-start | bytes 1572872 | tf_op jit(solution)/shard_map/ppermute | solution.py:312
  36.7 0.0 copy-start
  36.7 2.0 %copy-done = bf16[27,2,32,1024]{3,2,1,0:T(8,128)(2,1)S(1)} copy-done((bf16[27,2,32,1024]{3,2,1,0:T(8,128)(2,1)S(1)}, bf16[27,2,32,1024]{3,2,1,0:T(8,128)(2,1)}, u32[]{:S(2)}) %copy-start) | copy-done | bytes 3538968
  38.7 0.0 copy-start.1
  38.7 3.1 %own_half.1 = (f32[4,4,64,128]{3,2,1,0:T(8,128)S(1)}, bf16[3,576,512]{2,1,0:T(8,128)(2,1)S(1)}) custom-call(s32[1]{0:T(128)} %bitcast.4.half_ref, bf16[16,4,32,128]{3,2,1,0:T(8,128)(2,1)S(1)} %bitcast.8, bf16[3,576,1024]{2,1,0:T(8,128)(2,1)S(1)} %bitcast.6), custom_call_target="tpu_custom_call" | custom-call | flops 1073741824 | bytes 6291456 | tf_op jit(solution)/shard_map/own_half/pallas_call | solution.py:67
  41.8 1.7 %collective-permute-done.other_ref = bf16[16,4,32,128]{3,2,1,0:T(8,128)(2,1)S(1)} collective-permute-done((bf16[16,4,32,128]{3,2,1,0:T(8,128)(2,1)S(1)}, bf16[16,4,32,128]{3,2,1,0:T(8,128)(2,1)S(1)}, u32[]{:S(2)}, u32[]{:S(2)}) %collective-permute-start) | collective-permute-done | bytes 524320 | tf_op jit(solution)/shard_map/ppermute | solution.py:312
  43.5 1.3 %other_half.1 = (f32[2,2,64,128]{3,2,1,0:T(8,128)S(1)}, f32[2,2,64,128]{3,2,1,0:T(8,128)S(1)}, f32[2,2,64,128]{3,2,1,0:T(8,128)S(1)}, f32[2,2,64,128]{3,2,1,0:T(8,128)S(1)}) custom-call(bf16[16,4,32,128]{3,2,1,0:T(8,128)(2,1)S(1)} %collective-permute-done.other_ref, bf16[3,576,512]{2,1,0:T(8,128)(2,1)S(1)} %get-tuple-element.13.rest_ref, ...), custom_call_target="tpu_custom_call" | custom-call | flops 1073741824 | bytes 3145728 | tf_op jit(solution)/shard_map/other_half/pallas_call | solution.py:115
  44.7 12.4 %collective-permute-start.1 = (f32[2,2,64,128]{3,2,1,0:T(8,128)S(1)}, f32[2,2,64,128]{3,2,1,0:T(8,128)S(1)}, u32[]{:S(2)}, u32[]{:S(2)}) collective-permute-start(f32[2,2,64,128]{3,2,1,0:T(8,128)S(1)} %get-tuple-element.16), channel_id=1, source_target_pairs={{0,32},{32,64},{64,96},{96,0},{1,33},{33,65},{65,97},{97,1},{2,34}... | collective-permute-start | bytes 393224 | tf_op jit(solution)/shard_map/ppermute | solution.py:319
  57.1 3.2 %collective-permute-start.2 = (f32[2,2,64,128]{3,2,1,0:T(8,128)S(1)}, f32[2,2,64,128]{3,2,1,0:T(8,128)S(1)}, u32[]{:S(2)}, u32[]{:S(2)}) collective-permute-start(f32[2,2,64,128]{3,2,1,0:T(8,128)S(1)} %get-tuple-element.17), channel_id=1, source_target_pairs={{0,128},{128,256},{256,384},{384,0},{1,129},{129,257},{257,385},{3... | collective-permute-start | bytes 393224 | tf_op jit(solution)/shard_map/ppermute | solution.py:318
  60.3 3.2 %collective-permute-start.3 = (f32[2,2,64,128]{3,2,1,0:T(8,128)S(1)}, f32[2,2,64,128]{3,2,1,0:T(8,128)S(1)}, u32[]{:S(2)}, u32[]{:S(2)}) collective-permute-start(f32[2,2,64,128]{3,2,1,0:T(8,128)S(1)} %get-tuple-element.18), channel_id=1, source_target_pairs={{0,160},{32,192},{64,224},{96,128},{128,288},{160,320},{192,352},{... | collective-permute-start | bytes 393224 | tf_op jit(solution)/shard_map/ppermute | solution.py:317
  63.6 0.0 collective-permute-done.1.y_ref
  63.6 1.3 %collective-permute-done.2.z_ref = f32[2,2,64,128]{3,2,1,0:T(8,128)S(1)} collective-permute-done((f32[2,2,64,128]{3,2,1,0:T(8,128)S(1)}, f32[2,2,64,128]{3,2,1,0:T(8,128)S(1)}, u32[]{:S(2)}, u32[]{:S(2)}) %collective-permute-start.2) | collective-permute-done | bytes 131104 | tf_op jit(solution)/shard_map/ppermute | solution.py:318
  64.8 3.8 %collective-permute-done.3.corner_ref = f32[2,2,64,128]{3,2,1,0:T(8,128)S(1)} collective-permute-done((f32[2,2,64,128]{3,2,1,0:T(8,128)S(1)}, f32[2,2,64,128]{3,2,1,0:T(8,128)S(1)}, u32[]{:S(2)}, u32[]{:S(2)}) %collective-permute-start.3) | collective-permute-done | bytes 131104 | tf_op jit(solution)/shard_map/ppermute | solution.py:317
  68.6 0.1 gate.1
  68.8 22.7 %all_to_all.10.parts_ref = bf16[32,4,128]{2,1,0:T(4,128)(2,1)S(1)} all-to-all(bf16[32,4,128]{2,1,0:T(4,128)(2,1)S(1)} %gate.1), channel_id=1, replica_groups=mesh['gz'=4,'gy'=4,'ring'=16,'half'=2] {'ring','half'}, dimensions={0} | all-to-all | bytes 65536 | tf_op jit(solution)/shard_map/all_to_all | solution.py:321
  91.5 0.0 copy-done.1
  91.5 0.4 project.1
  92.0 10.4 %all_to_all.11.got_ref = bf16[16,3,16,128]{3,2,1,0:T(8,128)(2,1)S(1)} all-to-all(bf16[16,3,16,128]{3,2,1,0:T(8,128)(2,1)S(1)} %get-tuple-element.20), channel_id=1, replica_groups=mesh['gz'=4,'gy'=4,'ring'=16,'half'=2] {'gz','gy'}, dimensions={0} | all-to-all | bytes 393216 | tf_op jit(solution)/shard_map/all_to_all | solution.py:323
  102.4 0.7 lift.1
Async XLA Ops:
  32.0 11.4 %collective-permute-start = (bf16[16,4,32,128]{3,2,1,0:T(8,128)(2,1)S(1)}, bf16[16,4,32,128]{3,2,1,0:T(8,128)(2,1)S(1)}, u32[]{:S(2)}, u32[]{:S(2)}) collective-permute-start(bf16[16,4,32,128]{3,2,1,0:T(8,128)(2,1)S(1)} %bitcast.7), channel_id=1, source_target_pairs={{0,1},{1,0},{2,3},{3,2},{4,5},{5,4},{6,7},{7,6},{8,9},{9,8},{10,11... | collective-permute-start | bytes 1572872 | tf_op jit(solution)/shard_map/ppermute | solution.py:312
  36.7 2.0 %copy-start = (bf16[27,2,32,1024]{3,2,1,0:T(8,128)(2,1)S(1)}, bf16[27,2,32,1024]{3,2,1,0:T(8,128)(2,1)}, u32[]{:S(2)}) copy-start(bf16[27,2,32,1024]{3,2,1,0:T(8,128)(2,1)} %param.4) | copy-start | bytes 10616836
  38.7 52.8 %copy-start.1 = (bf16[1024,512]{1,0:T(8,128)(2,1)S(1)}, bf16[1024,512]{1,0:T(8,128)(2,1)}, u32[]{:S(2)}) copy-start(bf16[1024,512]{1,0:T(8,128)(2,1)} %proj_ref.1) | copy-start | bytes 3145732
  44.7 18.9 %collective-permute-start.1 = (f32[2,2,64,128]{3,2,1,0:T(8,128)S(1)}, f32[2,2,64,128]{3,2,1,0:T(8,128)S(1)}, u32[]{:S(2)}, u32[]{:S(2)}) collective-permute-start(f32[2,2,64,128]{3,2,1,0:T(8,128)S(1)} %get-tuple-element.16), channel_id=1, source_target_pairs={{0,32},{32,64},{64,96},{96,0},{1,33},{33,65},{65,97},{97,1},{2,34}... | collective-permute-start | bytes 393224 | tf_op jit(solution)/shard_map/ppermute | solution.py:319
  57.1 7.7 %collective-permute-start.2 = (f32[2,2,64,128]{3,2,1,0:T(8,128)S(1)}, f32[2,2,64,128]{3,2,1,0:T(8,128)S(1)}, u32[]{:S(2)}, u32[]{:S(2)}) collective-permute-start(f32[2,2,64,128]{3,2,1,0:T(8,128)S(1)} %get-tuple-element.17), channel_id=1, source_target_pairs={{0,128},{128,256},{256,384},{384,0},{1,129},{129,257},{257,385},{3... | collective-permute-start | bytes 393224 | tf_op jit(solution)/shard_map/ppermute | solution.py:318
  60.3 8.3 %collective-permute-start.3 = (f32[2,2,64,128]{3,2,1,0:T(8,128)S(1)}, f32[2,2,64,128]{3,2,1,0:T(8,128)S(1)}, u32[]{:S(2)}, u32[]{:S(2)}) collective-permute-start(f32[2,2,64,128]{3,2,1,0:T(8,128)S(1)} %get-tuple-element.18), channel_id=1, source_target_pairs={{0,160},{32,192},{64,224},{96,128},{128,288},{160,320},{192,352},{... | collective-permute-start | bytes 393224 | tf_op jit(solution)/shard_map/ppermute | solution.py:317

commit v8 on v6

--- a/solution.py
+++ b/solution.py
@@ -83,33 +83,82 @@
     )(half, own, weight)
 
 
-def other_half_kernel(other_ref, rest_ref, total_ref, keep_ref, y_ref, z_ref, corner_ref, cells):
+def add_products(products, step, first_dy, rows, sides, wanted):
+    for at, dy in enumerate(range(first_dy, first_dy + products.shape[0] // 192)):
+        for i, row in enumerate(rows):
+            z, y = row // 2 + 2 - step, row % 2 + 2 - dy
+            if wanted(z, y):
+                for dx in range(3):
+                    sides[dx, z, y] += products[
+                        (at * 3 + dx) * 64 : (at * 3 + dx + 1) * 64, i * 128 : (i + 1) * 128
+                    ]
+
+
+def summed(total_ref, sides, z, y):
+    lane = lax.broadcasted_iota(jnp.int32, (64, 128), 1)
+    return (
+        total_ref[z, y]
+        + sides[1, z, y]
+        + jnp.where(lane == 0, 0.0, pltpu.roll(sides[0, z, y], 1, 1))
+        + jnp.where(lane == 127, 0.0, pltpu.roll(sides[2, z, y], 127, 1))
+    )
+
+
+def other_half_kernel(other_ref, rest_ref, total_ref, cells, y_ref, z_ref, corner_ref, sides):
     for k in range(16):
         for row in range(4):
             cells[place_of(k), :, row * 128 : (row + 1) * 128] = other_ref[k, row]
-    sums = ((keep_ref, y_ref), (z_ref, corner_ref))
-    for z in range(4):
-        for y in range(4):
-            sums[z // 2][y // 2][z % 2, y % 2] = total_ref[z, y]
-    lane = lax.broadcasted_iota(jnp.int32, (64, 128), 1)
+    sides[...] = jnp.zeros_like(sides)
     for step in range(3):
-        products = jnp.dot(rest_ref[step], cells[...].reshape(512, 512), preferred_element_type=F32)
-        for z, y, term in spread_terms(products, lane):
-            z = z - step
-            sums[z // 2][y // 2][z % 2, y % 2] += term
+        count = 384 if step == 2 else 576
+        products = jnp.dot(
+            rest_ref[step, :count], cells[...].reshape(512, 512), preferred_element_type=F32
+        )
+        add_products(products, step, 0, range(4), sides, lambda z, y: z > 1 or y > 1)
+    for ref, top, left in ((y_ref, 0, 2), (z_ref, 2, 0), (corner_ref, 2, 2)):
+        for z in range(2):
+            for y in range(2):
+                ref[z, y] = summed(total_ref, sides, top + z, left + y)
+
+
+def kept_kernel(cells, rest_ref, total_ref, keep_ref, sides):
+    sides[...] = jnp.zeros_like(sides)
+    for step, rows in ((1, (0, 1)), (2, (0, 1, 2, 3))):
+        products = jnp.dot(
+            rest_ref[step, 192:],
+            cells[:, :, : len(rows) * 128].reshape(512, len(rows) * 128),
+            preferred_element_type=F32,
+        )
+        add_products(products, step, 1, rows, sides, lambda z, y: z < 2 and y < 2)
+    for z in range(2):
+        for y in range(2):
+            keep_ref[z, y] = summed(total_ref, sides, z, y)
 
 
 def other_half(other, rest, total):
-    return pl.pallas_call(
+    piece = jax.ShapeDtypeStruct((2, 2, 64, 128), F32)
+    params = pltpu.CompilerParams(vmem_limit_bytes=16 << 20)
+    cells, to_y, to_z, to_corner = pl.pallas_call(
         other_half_kernel,
         in_specs=[VMEM] * 3,
         out_specs=[VMEM] * 4,
-        out_shape=[jax.ShapeDtypeStruct((2, 2, 64, 128), F32)] * 4,
-        scratch_shapes=[pltpu.VMEM((16, 32, 512), BF16)],
-        compiler_params=pltpu.CompilerParams(vmem_limit_bytes=16 << 20),
+        out_shape=[jax.ShapeDtypeStruct((16, 32, 512), BF16), piece, piece, piece],
+        scratch_shapes=[pltpu.VMEM((3, 4, 4, 64, 128), F32)],
+        compiler_params=params,
         cost_estimate=pl.CostEstimate(flops=1 << 30, bytes_accessed=3 << 20, transcendentals=0),
         name="other_half",
     )(other, rest, total)
+    keep = pl.pallas_call(
+        kept_kernel,
+        in_specs=[VMEM] * 3,
+        out_specs=VMEM,
+        out_shape=piece,
+        scratch_shapes=[pltpu.VMEM((3, 2, 2, 64, 128), F32)],
+        compiler_params=params,
+        cost_estimate=pl.CostEstimate(flops=1 << 29, bytes_accessed=2 << 20, transcendentals=0),
+        name="kept",
+    )(cells, rest, total)
+    return keep, to_y, to_z, to_corner
 
 
 def gate_kernel(gz_ref, gy_ref, keep_ref, y_ref, z_ref, corner_ref, out_ref, turned):
@@ -296,7 +345,7 @@
 def on_device(volume, conv_weight, proj_weight):
     half = lax.axis_index("half")
     gz, gy = (lax.axis_index(axis).reshape(1) for axis in ("gz", "gy"))
-    own = lax.all_gather(volume.reshape(4, 32, 128), "ring", axis=0, tiled=False)
+    own = lax.all_gather(volume.reshape(128, 128), "ring", axis=0, tiled=True).reshape(16, 4, 32, 128)
     other = lax.ppermute(own, "half", [(0, 1), (1, 0)])
     total, rest = own_half(half.reshape(1), own, conv_weight.reshape(3, 576, 1024))
     keep, to_y, to_z, to_corner = other_half(other, rest, total)

time: 103 us -> 108 us (1.049)
  local copies, waits for them, and re-layouts: 2 us -> 5.68 us
  Pallas kernels: 5.72 us -> 7.76 us
  waiting for transfers between devices: 6.73 us -> 5.44 us
    unnamed x4 -> x12, local copies, waits for them, and re-layouts: 2 us -> 5.68 us
    ppermute x1, waiting for transfers between devices: 1.25 us -> 0.01 us  [on_device(): from_z = lax.ppermute(to_z, 'gz', step)]
  transfers between devices with their start and end apart: 4 -> 4, of which waited for: 3 -> 2; matrix products, arithmetic and copies ran while one was open for 0% -> 0% of each run, Pallas kernels for 3% -> 3%
where the time goes in v8:
time: 108 us
  blocking collectives  65.2 us (60%)
  starting transfers between devices  23.4 us (22%)
  Pallas kernels  7.76 us (7%)
  local copies, waits for them, and re-layouts  5.68 us (5%)
  waiting for transfers between devices  5.44 us (5%)
    all_gather x1, blocking collectives, on_device(): lax.all_gather(volume.reshape(128, 128), 'ring', axis=0, tiled=True)  32 us
    all_to_all x1, blocking collectives, on_device(): lax.all_to_all(sent, ('ring', 'half'), split_axis=0, concat_axis=0, tiled...  22.7 us
    ppermute x1, starting transfers between devices, on_device(): from_y = lax.ppermute(to_y, 'gy', step)  12.4 us
    all_to_all x1, blocking collectives, on_device(): lax.all_to_all(messages, ('gz', 'gy'), split_axis=0, concat_axis=0, tiled...  10.4 us
    unnamed x12, local copies, waits for them, and re-layouts  5.68 us
    ppermute x1, starting transfers between devices, on_device(): other = lax.ppermute(own, 'half', [(0, 1), (1, 0)])  4.64 us
    ppermute x1, waiting for transfers between devices, on_device(): from_corner = lax.ppermute(to_corner, ('gz', 'gy'), both)  3.77 us
    ppermute x1, starting transfers between devices, on_device(): from_corner = lax.ppermute(to_corner, ('gz', 'gy'), both)  3.21 us
  transfers between devices with their start and end apart: 4, of which 2 were waited for; matrix products, arithmetic and copies ran while one was open for 0% of the time, Pallas kernels for 3%

profile of v8, /device:TPU:1, one launch (start us, length us, event | category | flops | bytes accessed | tf_op | source)
XLA Modules:
  0.0 107.6 jit_solution(13560971290221427707)
XLA Ops:
  0.0 32.0 %all_gather.3 = bf16[2048,128]{1,0:T(8,128)(2,1)S(1)} all-gather(bf16[128,128]{1,0:T(8,128)(2,1)} %bitcast.9), channel_id=1, replica_groups=mesh['gz'=4,'gy'=4,'ring'=16,'half'=2] {'ring'}, dimensions={0}, use_global_device_ids=true | all-gather | bytes 557056 | tf_op jit(solution)/shard_map/all_gather | solution.py:348
  32.0 4.6 %collective-permute-start = (bf16[16,4,32,128]{3,2,1,0:T(8,128)(2,1)S(1)}, bf16[16,4,32,128]{3,2,1,0:T(8,128)(2,1)S(1)}, u32[]{:S(2)}, u32[]{:S(2)}) collective-permute-start(bf16[16,4,32,128]{3,2,1,0:T(8,128)(2,1)S(1)} %bitcast.7), channel_id=1, source_target_pairs={{0,1},{1,0},{2,3},{3,2},{4,5},{5,4},{6,7},{7,6},{8,9},{9,8},{10,11... | collective-permute-start | bytes 1572872 | tf_op jit(solution)/shard_map/ppermute | solution.py:349
  36.7 0.0 copy-start
  36.7 2.0 %copy-done = bf16[27,2,32,1024]{3,2,1,0:T(8,128)(2,1)S(1)} copy-done((bf16[27,2,32,1024]{3,2,1,0:T(8,128)(2,1)S(1)}, bf16[27,2,32,1024]{3,2,1,0:T(8,128)(2,1)}, u32[]{:S(2)}) %copy-start) | copy-done | bytes 3538968
  38.7 3.1 %own_half.1 = (f32[4,4,64,128]{3,2,1,0:T(8,128)S(1)}, bf16[3,576,512]{2,1,0:T(8,128)(2,1)S(1)}) custom-call(s32[1]{0:T(128)} %bitcast.4.half_ref, bf16[16,4,32,128]{3,2,1,0:T(8,128)(2,1)S(1)} %bitcast.8, bf16[3,576,1024]{2,1,0:T(8,128)(2,1)S(1)} %bitcast.6), custom_call_target="tpu_custom_call" | custom-call | flops 1073741824 | bytes 6291456 | tf_op jit(solution)/shard_map/own_half/pallas_call | solution.py:67
  41.8 1.7 %collective-permute-done.other_ref = bf16[16,4,32,128]{3,2,1,0:T(8,128)(2,1)S(1)} collective-permute-done((bf16[16,4,32,128]{3,2,1,0:T(8,128)(2,1)S(1)}, bf16[16,4,32,128]{3,2,1,0:T(8,128)(2,1)S(1)}, u32[]{:S(2)}, u32[]{:S(2)}) %collective-permute-start) | collective-permute-done | bytes 524320 | tf_op jit(solution)/shard_map/ppermute | solution.py:349
  43.5 0.8 copy-done.4
  44.3 1.0 copy-done.5
  45.3 1.8 %other_half.1 = (bf16[16,32,512]{2,1,0:T(8,128)(2,1)S(1)}, f32[2,2,64,128]{3,2,1,0:T(8,128)}, f32[2,2,64,128]{3,2,1,0:T(8,128)}, f32[2,2,64,128]{3,2,1,0:T(8,128)}) custom-call(bf16[16,4,32,128]{3,2,1,0:T(8,128)(2,1)S(1)} %copy-done.5, bf16[3,576,512]{2,1,0:T(8,128)(2,1)S(1)} %get-tuple-element.13.rest_ref, f32[4,4,64,128]{3,2,1,0:T(8,128)S(1)} %get-tuple-element.14.total_ref), custom_call_target="tpu_custom_call" | custom-call | flops 1073741824 | bytes 3145728 | tf_op jit(solution)/shard_map/other_half/pallas_call | solution.py:141
  47.1 0.8 copy-done.2
  47.9 12.4 %collective-permute-start.1 = (f32[2,2,64,128]{3,2,1,0:T(8,128)}, f32[2,2,64,128]{3,2,1,0:T(8,128)S(1)}, u32[]{:S(2)}, u32[]{:S(2)}) collective-permute-start(f32[2,2,64,128]{3,2,1,0:T(8,128)} %get-tuple-element.16), channel_id=1, source_target_pairs={{0,32},{32,64},{64,96},{96,0},{1,33},{33,65},{65,97},{97,1},{2,34}... | collective-permute-start | bytes 393224 | tf_op jit(solution)/shard_map/ppermute | solution.py:356
  60.3 3.2 %collective-permute-start.2 = (f32[2,2,64,128]{3,2,1,0:T(8,128)}, f32[2,2,64,128]{3,2,1,0:T(8,128)}, u32[]{:S(2)}, u32[]{:S(2)}) collective-permute-start(f32[2,2,64,128]{3,2,1,0:T(8,128)} %get-tuple-element.17), channel_id=1, source_target_pairs={{0,128},{128,256},{256,384},{384,0},{1,129},{129,257},{257,385},{3... | collective-permute-start | bytes 393224 | tf_op jit(solution)/shard_map/ppermute | solution.py:355
  63.5 3.2 %collective-permute-start.3 = (f32[2,2,64,128]{3,2,1,0:T(8,128)}, f32[2,2,64,128]{3,2,1,0:T(8,128)}, u32[]{:S(2)}, u32[]{:S(2)}) collective-permute-start(f32[2,2,64,128]{3,2,1,0:T(8,128)} %get-tuple-element.18), channel_id=1, source_target_pairs={{0,160},{32,192},{64,224},{96,128},{128,288},{160,320},{192,352},{... | collective-permute-start | bytes 393224 | tf_op jit(solution)/shard_map/ppermute | solution.py:354
  66.8 0.0 copy-start.3
  66.8 1.0 copy-done.3
  67.8 0.6 kept.1.keep_ref
  68.4 0.0 collective-permute-done.1.y_ref
  68.4 0.0 collective-permute-done.2.z_ref
  68.4 3.8 %collective-permute-done.3.corner_ref = f32[2,2,64,128]{3,2,1,0:T(8,128)} collective-permute-done((f32[2,2,64,128]{3,2,1,0:T(8,128)}, f32[2,2,64,128]{3,2,1,0:T(8,128)}, u32[]{:S(2)}, u32[]{:S(2)}) %collective-permute-start.3) | collective-permute-done | bytes 131104 | tf_op jit(solution)/shard_map/ppermute | solution.py:354
  72.2 1.1 %gate.1 = bf16[32,4,128]{2,1,0:T(4,128)(2,1)S(1)} custom-call(s32[1]{0:T(128)} %bitcast.gz_ref, s32[1]{0:T(128)} %bitcast.1.gy_ref, f32[2,2,64,128]{3,2,1,0:T(8,128)S(1)} %kept.1.keep_ref, f32[2,2,64,128]{3,2,1,0:T(8,128)S(1)} %collective-permute-done.1.y_ref, f32[2,2,64,128]{3,2,1,0:T(8,128)} %collective-permute-done.2.z_ref, ...), custom_call_target="tpu_custom_call" | custom-call | tf_op jit(solution)/shard_map/gate/pallas_call | solution.py:185
  73.3 22.7 %all_to_all.10.parts_ref = bf16[32,4,128]{2,1,0:T(4,128)(2,1)S(1)} all-to-all(bf16[32,4,128]{2,1,0:T(4,128)(2,1)S(1)} %gate.1), channel_id=1, replica_groups=mesh['gz'=4,'gy'=4,'ring'=16,'half'=2] {'ring','half'}, dimensions={0} | all-to-all | bytes 65536 | tf_op jit(solution)/shard_map/all_to_all | solution.py:358
  96.0 0.4 project.1
  96.4 10.4 %all_to_all.11.got_ref = bf16[16,3,16,128]{3,2,1,0:T(8,128)(2,1)S(1)} all-to-all(bf16[16,3,16,128]{3,2,1,0:T(8,128)(2,1)S(1)} %get-tuple-element.20), channel_id=1, replica_groups=mesh['gz'=4,'gy'=4,'ring'=16,'half'=2] {'gz','gy'}, dimensions={0} | all-to-all | bytes 393216 | tf_op jit(solution)/shard_map/all_to_all | solution.py:360
  106.9 0.7 lift.1
  (5 shorter events, 0.0 us)
Async XLA Ops:
  32.0 11.4 %collective-permute-start = (bf16[16,4,32,128]{3,2,1,0:T(8,128)(2,1)S(1)}, bf16[16,4,32,128]{3,2,1,0:T(8,128)(2,1)S(1)}, u32[]{:S(2)}, u32[]{:S(2)}) collective-permute-start(bf16[16,4,32,128]{3,2,1,0:T(8,128)(2,1)S(1)} %bitcast.7), channel_id=1, source_target_pairs={{0,1},{1,0},{2,3},{3,2},{4,5},{5,4},{6,7},{7,6},{8,9},{9,8},{10,11... | collective-permute-start | bytes 1572872 | tf_op jit(solution)/shard_map/ppermute | solution.py:349
  36.7 2.0 %copy-start = (bf16[27,2,32,1024]{3,2,1,0:T(8,128)(2,1)S(1)}, bf16[27,2,32,1024]{3,2,1,0:T(8,128)(2,1)}, u32[]{:S(2)}) copy-start(bf16[27,2,32,1024]{3,2,1,0:T(8,128)(2,1)} %param.4) | copy-start | bytes 10616836
  43.5 0.8 copy-start.4
  44.3 1.0 copy-start.5
  45.3 50.7 %copy-start.1 = (bf16[1024,512]{1,0:T(8,128)(2,1)S(1)}, bf16[1024,512]{1,0:T(8,128)(2,1)}, u32[]{:S(2)}) copy-start(bf16[1024,512]{1,0:T(8,128)(2,1)} %proj_ref.1) | copy-start | bytes 3145732
  47.1 0.8 copy-start.2
  47.9 20.4 %collective-permute-start.1 = (f32[2,2,64,128]{3,2,1,0:T(8,128)}, f32[2,2,64,128]{3,2,1,0:T(8,128)S(1)}, u32[]{:S(2)}, u32[]{:S(2)}) collective-permute-start(f32[2,2,64,128]{3,2,1,0:T(8,128)} %get-tuple-element.16), channel_id=1, source_target_pairs={{0,32},{32,64},{64,96},{96,0},{1,33},{33,65},{65,97},{97,1},{2,34}... | collective-permute-start | bytes 393224 | tf_op jit(solution)/shard_map/ppermute | solution.py:356
  60.3 8.1 %collective-permute-start.2 = (f32[2,2,64,128]{3,2,1,0:T(8,128)}, f32[2,2,64,128]{3,2,1,0:T(8,128)}, u32[]{:S(2)}, u32[]{:S(2)}) collective-permute-start(f32[2,2,64,128]{3,2,1,0:T(8,128)} %get-tuple-element.17), channel_id=1, source_target_pairs={{0,128},{128,256},{256,384},{384,0},{1,129},{129,257},{257,385},{3... | collective-permute-start | bytes 393224 | tf_op jit(solution)/shard_map/ppermute | solution.py:355
  63.5 8.6 %collective-permute-start.3 = (f32[2,2,64,128]{3,2,1,0:T(8,128)}, f32[2,2,64,128]{3,2,1,0:T(8,128)}, u32[]{:S(2)}, u32[]{:S(2)}) collective-permute-start(f32[2,2,64,128]{3,2,1,0:T(8,128)} %get-tuple-element.18), channel_id=1, source_target_pairs={{0,160},{32,192},{64,224},{96,128},{128,288},{160,320},{192,352},{... | collective-permute-start | bytes 393224 | tf_op jit(solution)/shard_map/ppermute | solution.py:354
  66.8 1.0 copy-start.3
